TPU v7x, 128 devices: a whole 4x4x4 slice. The times are simulated.
128 devices in a mesh: gx: 8 (over x, z_hi), gy: 16 (over y, z_lo, core).
Axes of the slice: x: 4, y: 4, z: 4 (z_hi: 2, z_lo: 2; z = z_hi * 2 + z_lo), core: 2. Of those that a mesh axis runs over, the one named last changes fastest.
Arguments:
- adjoint_vel: float32 [512, 2, 62, 32, 128], P(('gx', 'gy')), may hold values from -6 to 6
- velocity: bfloat16 [512, 2, 62, 32, 128], P(('gx', 'gy')), may hold values from -6 to 6
- drag_coef: float32 [512, 32, 128], P(('gx', 'gy')), may hold values from 0.3 to 3
- level_count: int32 [512, 32, 128], P(('gx', 'gy')), may hold values from 1 to 62
- block_ids: int32 [512], P(('gx', 'gy')), may hold values from 0 to 256, as said below
- bathymetry: float32 [512, 2048], P('gy', 'gx'), may hold values from 0.25 to 1
- land_mask: int32 [512, 2048], P('gy', 'gx'), may hold values 0 or 1
Outputs:
- corrected_adjoint: float32 [512, 2, 62, 32, 128], P(('gx', 'gy'))
- drag_gradient: float32 [512, 32, 128], P(('gx', 'gy'))
- surface_height: float32 [512, 2048], P('gy', 'gx')
- bathy_sensitivity: float32 [512, 2048], P('gy', 'gx')
Inputs may be any that keep to these rules, and one draw needn't show every extreme that they name: `block_ids`: each device's 4 entries name the blocks it holds, then 256 in unused slots; each block number below 256 appears exactly once over all devices; each device holds 1 to 4 blocks, and some device holds 4.
All inputs are finite; a program needn't handle non-finite values. No bound on the sum of `land_mask` on one device may be relied on, other than what follows from the above.
Results may differ from a plain program's by a relative error of at most 0.0003.
Values sent between devices are 32-bit elements; how exact they have to be, the bound alone decides.
A program may use at most 128 MiB of HBM per device.

v0:
```python
import jax
import jax.numpy as jnp
from jax import lax
from jax.sharding import PartitionSpec as P

STEPS = 32


mix_rate = 0.25
mix_sweeps = 2
drag_step = 0.5
force_scale = 0.25
pressure_gain = 0.5
surface_shift = 1.0 / 64.0
speed_floor = 0.01


def padded(cells, sides, width):
    for axis, dim in sides:
        count = lax.axis_size(axis)
        ends = count - 1
        head = lax.slice_in_dim(cells, 0, width, axis=dim)
        tail = lax.slice_in_dim(cells, cells.shape[dim] - width, cells.shape[dim], axis=dim)
        cells = jnp.concatenate(
            [
                lax.ppermute(tail, axis, [(i, (i + 1) % count) for i in range(ends)]),
                cells,
                lax.ppermute(head, axis, [((i + 1) % count, i) for i in range(ends)]),
            ],
            axis=dim,
        )
    return cells


def chebyshev_table(total_steps):
    highest = surface_shift + 8.0
    centre = 0.5 * (highest + surface_shift)
    radius = 0.5 * (highest - surface_shift)
    sigma_ratio = centre / radius
    ratio_prev = 1.0 / sigma_ratio
    table = []
    for _ in range(total_steps):
        ratio_next = 1.0 / (2.0 * sigma_ratio - ratio_prev)
        table.append((ratio_next * ratio_prev, 2.0 * ratio_next / radius))
        ratio_prev = ratio_next
    return (centre, table)


def column_block(adjoint, velocity, drag, levels):
    depth_index = lax.broadcasted_iota(jnp.int32, adjoint.shape[1:], 0)
    wetness = (depth_index < levels[None]).astype(jnp.float32)
    forcing = force_scale * jnp.sum(wetness[None] * adjoint, axis=(0, 1))
    column_field = adjoint * wetness[None]
    wet_below = wetness[None, 1:]
    for _ in range(mix_sweeps):
        level_flux = mix_rate * (column_field[:, 1:] - column_field[:, :-1]) * wet_below
        zeros_row = jnp.zeros_like(column_field[:, :1])
        column_field = (
            column_field
            + jnp.concatenate([level_flux, zeros_row], axis=1)
            - jnp.concatenate([zeros_row, level_flux], axis=1)
        )
    bottom = (depth_index == levels[None] - 1).astype(jnp.float32)
    flow_all = velocity.astype(jnp.float32)
    flow_bottom = jnp.sum(bottom[None] * flow_all, axis=1)
    field_bottom = jnp.sum(bottom[None] * column_field, axis=1)
    bottom_speed = jnp.sqrt(
        flow_bottom[0] * flow_bottom[0] + flow_bottom[1] * flow_bottom[1] + speed_floor
    )
    along_flow = flow_bottom[0] * field_bottom[0] + flow_bottom[1] * field_bottom[1]
    drag_pull = drag[None] * (
        bottom_speed[None] * field_bottom + flow_bottom * (along_flow / bottom_speed)[None]
    )
    mixed_field = column_field - drag_step * bottom[None] * drag_pull[:, None]
    drag_grad = -drag_step * bottom_speed * along_flow
    return (mixed_field, drag_grad, forcing, wetness)


def face_weights(scaled):
    east = jnp.sqrt(scaled[:, :-1] * scaled[:, 1:])
    north = jnp.sqrt(scaled[:-1, :] * scaled[1:, :])
    return (east, north)


def operate(values, east, north):
    east_flux = east * (values[:, :-1] - values[:, 1:])
    north_flux = north * (values[:-1, :] - values[1:, :])
    result = surface_shift * values
    result = result + jnp.pad(east_flux, ((0, 0), (0, 1))) - jnp.pad(east_flux, ((0, 0), (1, 0)))
    result = result + jnp.pad(north_flux, ((0, 1), (0, 0))) - jnp.pad(north_flux, ((1, 0), (0, 0)))
    return result


def surface_terms(height, scaled):
    east, north = face_weights(scaled)
    east_step = height[:, 1:] - height[:, :-1]
    north_step = height[1:, :] - height[:-1, :]
    east_energy = east * east_step * east_step
    north_energy = north * north_step * north_step
    total = (
        east_energy[1:-1, 1:]
        + east_energy[1:-1, :-1]
        + north_energy[1:, 1:-1]
        + north_energy[:-1, 1:-1]
    )
    sensitivity = 0.25 * total / jnp.maximum(scaled[1:-1, 1:-1], 0.25)
    return (height[1:-1, 1:-1], east_step[1:-1, 1:], north_step[1:, 1:-1], sensitivity)


def per_device(adjoint_vel, velocity, drag_coef, level_count, block_ids, bathymetry, land_mask):
    slots = block_ids.shape[0]
    rows_block = drag_coef.shape[1]
    cols_block = drag_coef.shape[2]
    lon_count = lax.axis_size("gx")
    lat_count = lax.axis_size("gy")
    my_lon = lax.axis_index("gx")
    my_lat = lax.axis_index("gy")
    device_count = lon_count * lat_count
    block_total = 2 * device_count
    my_device = my_lon * lat_count + my_lat
    mixed_field, drag_grad, forcing, wetness = jax.vmap(column_block)(
        adjoint_vel, velocity, drag_coef, level_count
    )
    valid = (block_ids < block_total).astype(jnp.float32)
    piece_forcing = lax.all_gather(forcing, ("gx", "gy"), axis=0, tiled=True)
    piece_ids = lax.all_gather(block_ids, ("gx", "gy"), axis=0, tiled=True)
    wanted = my_device * 2 + lax.broadcasted_iota(jnp.int32, (2, piece_ids.shape[0]), 0)
    selector = (wanted == piece_ids[None, :]).astype(jnp.float32)
    own_blocks = jnp.einsum("hn,nyx->hyx", selector, piece_forcing, precision=lax.Precision.HIGHEST)
    wet_mask = land_mask.astype(jnp.float32)
    scaled = bathymetry * wet_mask
    source = jnp.concatenate([own_blocks[0], own_blocks[1]], axis=1) * wet_mask
    centre, table = chebyshev_table(STEPS)
    scaled_cycle = padded(scaled, (("gx", 1), ("gy", 0)), 1)
    east, north = face_weights(scaled_cycle)
    coefs = jnp.array(table, jnp.float32)

    def advance(step_index, state):
        height, residual, direction = state
        direction_cycle = padded(direction, (("gx", 1), ("gy", 0)), 1)
        image = operate(direction_cycle, east, north)[1:-1, 1:-1]
        height = height + direction
        residual = residual - image
        direction = coefs[step_index, 0] * direction + coefs[step_index, 1] * residual
        return (height, residual, direction)

    height, residual, direction = lax.fori_loop(
        0, STEPS, advance, (jnp.zeros_like(source), source, source / centre)
    )
    height_cycle = padded(height, (("gx", 1), ("gy", 0)), 1)
    surface, east_step, north_step, sensitivity = surface_terms(height_cycle, scaled_cycle)
    gradients = jnp.stack([east_step, north_step])
    even_grads = gradients.reshape(2, rows_block, 2, cols_block).transpose(2, 0, 1, 3)
    piece = lax.all_gather(even_grads, ("gx", "gy"), axis=0, tiled=True)
    count_here = piece.shape[0]
    listed_here = lax.broadcasted_iota(jnp.int32, (slots, count_here), 1)
    selector = (block_ids[:, None] == listed_here).astype(jnp.float32)
    slot_grads = jnp.einsum("sn,ncyx->scyx", selector, piece, precision=lax.Precision.HIGHEST)
    corrected = valid[:, None, None, None, None] * (
        mixed_field - pressure_gain * wetness[:, None] * slot_grads[:, :, None]
    )
    return (corrected, drag_grad * valid[:, None, None], surface, sensitivity)


def solution(mesh):
    in_specs = (
        P(("gx", "gy"), None, None, None, None),
        P(("gx", "gy"), None, None, None, None),
        P(("gx", "gy"), None, None),
        P(("gx", "gy"), None, None),
        P(("gx", "gy")),
        P("gy", "gx"),
        P("gy", "gx"),
    )
    out_specs = (
        P(("gx", "gy"), None, None, None, None),
        P(("gx", "gy"), None, None),
        P("gy", "gx"),
        P("gy", "gx"),
    )
    return jax.shard_map(
        per_device, mesh=mesh, in_specs=in_specs, out_specs=out_specs, check_vma=False
    )
```

profile of v0, /device:TPU:1, one launch (start us, length us, event | category | flops | bytes accessed | tf_op | source)
XLA Modules:
  0.0 1145.3 jit_solution(12119561390605994278)
XLA Ops:
  8.6 9.6 fusion.33
  19.2 68.7 %all-reduce.8 = s32[512]{0:T(512)S(1)} all-reduce(s32[512]{0:T(512)S(1)} %dynamic-update-slice), channel_id=1, replica_groups=mesh['gx'=8,'gy'=16] {'gx','gy'}, use_global_device_ids=true, to_apply=%add.8 | all-reduce | flops 512 | bytes 4096
  87.9 136.0 %all-gather.3.cloned.1.call-done = f32[512,32,128]{2,1,0:T(8,128)} async-done(((f32[4,32,128]{2,1,0:T(8,128)}), f32[512,32,128]{2,1,0:T(8,128)}) %all-gather.3.cloned.1.call-update) | async-done | bytes 8388624 | tf_op jit(solution)/shard_map/all_gather | solution.py:125
  223.9 10.4 fusion.5
  253.7 626.0 %while.21 = (s32[]{:T(128)}, f32[32,256]{1,0:T(8,128)S(1)}, f32[32,256]{1,0:T(8,128)S(1)}, f32[32,256]{1,0:T(8,128)S(1)}, f32[34,257]{1,0:T(8,128)S(1)}, /*index...) while((s32[]{:T(128)}, f32[32,256]{1,0:T(8,128)S(1)}, ...), condition=%wide.region_4.5_spmd.clone.clone, body=%wide.region_3.4_spmd.sunk.clone.clone.sunk | while | flops 211823 | bytes 656747 | solution.py:147
  310.9 8.2 collective-permute-start.1
  330.5 8.2 collective-permute-start.1
  350.2 8.2 collective-permute-start.1
  369.8 8.2 collective-permute-start.1
  389.5 8.2 collective-permute-start.1
  409.2 8.2 collective-permute-start.1
  428.8 8.2 collective-permute-start.1
  448.5 8.2 collective-permute-start.1
  468.2 8.2 collective-permute-start.1
  487.8 8.2 collective-permute-start.1
  507.5 8.2 collective-permute-start.1
  527.2 8.2 collective-permute-start.1
  546.8 8.2 collective-permute-start.1
  566.5 8.2 collective-permute-start.1
  586.1 8.2 collective-permute-start.1
  605.8 8.2 collective-permute-start.1
  625.5 8.2 collective-permute-start.1
  664.8 8.2 collective-permute-start.1
  684.5 8.2 collective-permute-start.1
  841.8 8.2 collective-permute-start.1
  861.4 8.2 collective-permute-start.1
  909.4 8.9 fusion.8
  918.4 8.3 pad_subtract_fusion.3
  932.4 10.7 multiply_reduce_fusion
  948.9 165.9 %all-gather.5.cloned.1.call-done = f32[256,2,32,128]{3,2,1,0:T(8,128)} async-done(((f32[2,2,32,128]{3,2,1,0:T(8,128)}), f32[256,2,32,128]{3,2,1,0:T(8,128)}) %all-gather.5.cloned.1.call-update) | async-done | bytes 8388624 | tf_op jit(solution)/shard_map/all_gather | solution.py:154
  1114.8 10.6 fusion.3
  1125.4 13.1 %subtract_multiply_fusion = f32[4,2,62,32,128]{4,3,2,1,0:T(8,128)} fusion(f32[4,2,32,128]{3,2,1,0:T(8,128)S(1)} %copy.26, f32[4,62,32,128]{3,2,1,0:T(8,128)S(1)} %copy-done.3, f32[4,2,32,128]{3,2,1,0:T(8,128)S(1)} %add_multiply_fusion, f32[4,62,32,128]{3,2,1,0:T(8,128)S(1)} %copy-done.2, f32[4]{0:T(128)S(1)} %compare_convert_fusion, ...), kind=kLoop, calls=%fused_computation.22 | loop fusion | flops 14221312 | bytes 32636944 | tf_op jit(solution)/shard_map/mul | solution.py:159
  (540 shorter events, 514.5 us)
Async XLA Ops:
  7.2 216.7 %all-gather.3.cloned.1.call-start = ((), (), s32[]{:S(2)}) async-start(), calls=%async_computation | async-start | bytes 8454144 | tf_op jit(solution)/shard_map/all_gather | solution.py:125
  18.9 1095.9 %all-gather.5.cloned.1.call-start = ((), (), s32[]{:S(2)}) async-start(), calls=%async_computation.1 | async-start | bytes 8454144 | tf_op jit(solution)/shard_map/all_gather | solution.py:154
  290.0 9.4 collective-permute-start
  309.6 9.5 collective-permute-start
  329.2 9.5 collective-permute-start
  348.9 9.5 collective-permute-start
  368.6 9.5 collective-permute-start
  388.2 9.5 collective-permute-start
  407.9 9.5 collective-permute-start
  427.5 9.5 collective-permute-start
  447.2 9.5 collective-permute-start
  466.9 9.5 collective-permute-start
  486.5 9.5 collective-permute-start
  506.2 9.5 collective-permute-start
  525.9 9.5 collective-permute-start
  545.5 9.5 collective-permute-start
  565.2 9.5 collective-permute-start
  584.9 9.5 collective-permute-start
  604.5 9.5 collective-permute-start
  624.2 9.5 collective-permute-start
  643.8 9.5 collective-permute-start
  663.5 9.5 collective-permute-start
  683.2 9.5 collective-permute-start
  702.8 9.5 collective-permute-start
  722.5 9.5 collective-permute-start
  742.2 9.5 collective-permute-start
  761.8 9.5 collective-permute-start
  781.5 9.5 collective-permute-start
  801.1 9.5 collective-permute-start
  820.8 9.5 collective-permute-start
  840.5 9.5 collective-permute-start
  860.1 9.5 collective-permute-start
  (118 other events, 2065.1 us)
Sparse Core Ops, SparseCore 0:
  19.0 204.8 all-gather.2
  904.3 210.4 all-gather.4
where the time goes:
time: 1150 us
  starting transfers between devices  464 us (40%)
  waiting for transfers between devices  402 us (35%)
  other arithmetic  126 us (11%)
  blocking collectives  68.7 us (6%)
  local copies, waits for them, and re-layouts  46.9 us (4%)
  matrix products  21 us (2%)
  between operations  14.4 us (1%)
    ppermute x68, starting transfers between devices, padded(): lax.ppermute(tail, axis, [(i, (i + 1) % count) for i in range(ends)])  351 us
    all_gather x1, waiting for transfers between devices, per_device(): piece = lax.all_gather(even_grads, ('gx', 'gy'), axis=0, tiled=True)  166 us
    all_gather x1, waiting for transfers between devices, per_device(): piece_forcing = lax.all_gather(forcing, ('gx', 'gy'), axis=0, tiled=True)  136 us
    ppermute x68, starting transfers between devices, padded(): lax.ppermute(head, axis, [((i + 1) % count, i) for i in range(ends)])  113 us
    ppermute x68, waiting for transfers between devices, padded(): lax.ppermute(head, axis, [((i + 1) % count, i) for i in range(ends)])  72.6 us
    unnamed x1, blocking collectives  68.7 us
    add x32, other arithmetic, advance(): coefs[step_index, 0] * direction + coefs[step_index, 1] * residual  45.2 us
    dynamic_slice x32, local copies, waits for them, and re-layouts, advance(): coefs[step_index, 0] * direction + coefs[step_index, 1] * residual  43.3 us
  transfers between devices with their start and end apart: 138, of which 70 were waited for; matrix products, arithmetic and copies ran while one was open for 8% of the time, Pallas kernels for 0%

commit v1 on v0

v1 whole, which is shorter than its diff:
```python
import jax
import jax.numpy as jnp
from jax import lax
from jax.experimental import pallas as pl
from jax.experimental.pallas import tpu as pltpu
from jax.sharding import PartitionSpec as P

MESH = pl.DeviceIdType.MESH
STEPS = 32
LEV = 62
BY = 32
BX = 128
SLOTS = 4
HEIGHT_ROWS = 40
NX_CHIPS, NY_CHIPS, NZ_CHIPS, CORES = 4, 4, 4, 2
A_SIZE = NX_CHIPS * CORES
B_SIZE = NY_CHIPS * NZ_CHIPS
AROUND = ((-1, -1), (-1, 0), (-1, 1), (0, -1), (0, 1), (1, -1), (1, 0), (1, 1))

mix_rate = 0.25
drag_step = 0.5
force_scale = 0.25
pressure_gain = 0.5
surface_shift = 1.0 / 64.0
speed_floor = 0.01


def chebyshev_table(total_steps):
    highest = surface_shift + 8.0
    centre = 0.5 * (highest + surface_shift)
    radius = 0.5 * (highest - surface_shift)
    sigma_ratio = centre / radius
    ratio_prev = 1.0 / sigma_ratio
    table = []
    for _ in range(total_steps):
        ratio_next = 1.0 / (2.0 * sigma_ratio - ratio_prev)
        table.append((ratio_next * ratio_prev, 2.0 * ratio_next / radius))
        ratio_prev = ratio_next
    return (centre, table)


def forcing_kernel(levels_ref, adjoint_ref, forcing_ref):
    for row in range(0, BY, 8):
        levels = levels_ref[0, row : row + 8, :]
        total = jnp.zeros((8, BX), jnp.float32)
        for k in range(LEV):
            pair = adjoint_ref[0, 0, k, row : row + 8, :] + adjoint_ref[0, 1, k, row : row + 8, :]
            total = total + jnp.where(levels > k, pair, 0.0)
        forcing_ref[0, row : row + 8, :] = force_scale * total


def column_forcing(level_count, adjoint_vel):
    return pl.pallas_call(
        forcing_kernel,
        grid=(SLOTS,),
        in_specs=[
            pl.BlockSpec((1, BY, BX), lambda s: (s, 0, 0)),
            pl.BlockSpec((1, 2, LEV, BY, BX), lambda s: (s, 0, 0, 0, 0)),
        ],
        out_specs=pl.BlockSpec((1, BY, BX), lambda s: (s, 0, 0)),
        out_shape=jax.ShapeDtypeStruct((SLOTS, BY, BX), jnp.float32),
        name="column_forcing",
    )(level_count, adjoint_vel)


def lane_roll(values, shift):
    return pltpu.roll(values, shift % values.shape[-1], values.ndim - 1)


def surface_kernel(
    ids_ref,
    table_ref,
    forcing_ref,
    bathymetry_ref,
    mask_ref,
    grads_ref,
    surface_ref,
    sens_ref,
    idbuf,
    forward_vec,
    back_vec,
    forward_idx,
    back_idx,
    cand,
    spread,
    gathered,
    source_own,
    scaled_own,
    packed_scaled,
    packed_source,
    vert_scaled,
    vert_source,
    side_scaled,
    side_source,
    east_w,
    north_w,
    scaled_ext,
    direction,
    residual,
    height,
    blocks,
    returned,
    slot_out,
    slot_in,
    slot_sum,
    id_send,
    id_recv,
    a_send,
    a_recv,
    b_send,
    b_recv,
    h_send,
    h_recv,
    g_send,
    g_recv,
    rb_send,
    rb_recv,
    ra_send,
    ra_recv,
    local_sem,
):
    gx = lax.axis_index("gx")
    gy = lax.axis_index("gy")
    my_x, my_zh = lax.div(gx, 2), lax.rem(gx, 2)
    my_y, my_zl, my_c = lax.div(gy, 4), lax.rem(lax.div(gy, 2), 2), lax.rem(gy, 2)
    my_z = my_zh * 2 + my_zl

    def a_peer(o, sign):
        step_x, step_c = o // 2, o % 2
        if sign < 0:
            step_x = (NX_CHIPS - step_x) % NX_CHIPS
        x = lax.rem(my_x + step_x, NX_CHIPS)
        c = lax.rem(my_c + step_c, CORES)
        return (x * 2 + my_zh, my_y * 4 + my_zl * 2 + c)

    def b_peer(p, sign):
        step_y, step_z = p // NZ_CHIPS, p % NZ_CHIPS
        if sign < 0:
            step_y = (NY_CHIPS - step_y) % NY_CHIPS
            step_z = (NZ_CHIPS - step_z) % NZ_CHIPS
        y = lax.rem(my_y + step_y, NY_CHIPS)
        z = lax.rem(my_z + step_z, NZ_CHIPS)
        return (my_x * 2 + lax.div(z, 2), y * 4 + lax.rem(z, 2) * 2 + my_c)

    def near(n):
        dx, dy = AROUND[n]
        return (lax.rem(gx + dx + 8, 8), lax.rem(gy + dy + 16, 16))

    def copy(src, dst, send, recv, to):
        return pltpu.make_async_remote_copy(
            src_ref=src, dst_ref=dst, send_sem=send, recv_sem=recv, device_id=to, device_id_type=MESH
        )

    barrier = pltpu.get_barrier_semaphore()
    for o in range(1, A_SIZE):
        pl.semaphore_signal(barrier, inc=1, device_id=a_peer(o, 1), device_id_type=MESH)
    for p in range(1, B_SIZE):
        pl.semaphore_signal(barrier, inc=1, device_id=b_peer(p, 1), device_id_type=MESH)
    for n in range(8):
        pl.semaphore_signal(barrier, inc=1, device_id=near(n), device_id_type=MESH)

    lane8 = lax.broadcasted_iota(jnp.int32, (8, BX), 1)
    lane32 = lax.broadcasted_iota(jnp.int32, (BY, BX), 1)
    row32 = lax.broadcasted_iota(jnp.int32, (BY, BX), 0)

    id_row = jnp.full((8, BX), -1, jnp.int32)
    for s in range(SLOTS):
        id_row = jnp.where(lane8 == s, ids_ref[s], id_row)
    idbuf[0] = id_row
    cand[0] = jnp.zeros((BY, BX), jnp.float32)
    cand[1 : 1 + SLOTS] = forcing_ref[...]
    blank = jnp.zeros((HEIGHT_ROWS, BX), jnp.float32)
    returned[0] = blank

    def pack(block, base):
        out = jnp.zeros((8, BX), jnp.float32)
        for q in range(4):
            part = lane_roll(block[8 * q : 8 * q + 8, :], 32 * q - base)
            out = jnp.where(lane8 // 32 == q, part, out)
        return out

    def unpack(packed, base):
        return jnp.concatenate([lane_roll(packed, base - 32 * q) for q in range(4)], axis=0)

    wet = mask_ref[...].astype(jnp.float32)
    scaled = bathymetry_ref[...] * wet
    scaled_own[0] = scaled[:, :BX]
    scaled_own[1] = scaled[:, BX:]

    pl.semaphore_wait(barrier, A_SIZE - 1 + B_SIZE - 1 + 8)

    id_copies = [None] * A_SIZE
    a_copies = [None] * A_SIZE
    for o in range(1, A_SIZE):
        id_copies[o] = copy(idbuf.at[0], idbuf.at[o], id_send.at[o], id_recv.at[o], a_peer(o, 1))
        id_copies[o].start()
    for o in range(1, A_SIZE):
        a_copies[o] = copy(
            forcing_ref, cand.at[pl.ds(1 + SLOTS * o, SLOTS)], a_send.at[o], a_recv.at[o], a_peer(o, 1)
        )
        a_copies[o].start()

    def halo_copies(own, packed, vert, side, send, recv):
        copies = []
        for n, (dx, dy) in enumerate(AROUND):
            if dx == 0:
                src, dst = own, vert.at[0 if dy < 0 else 1]
            else:
                src, dst = packed.at[0 if dx < 0 else 1], side.at[n]
            copies.append(copy(src, dst, send.at[n], recv.at[n], near(n)))
        return copies

    def extended(own, vert, side):
        bands = []
        for dy in (-1, 0, 1):
            if dy == 0:
                left, right = own[0], own[1]
                inside = jnp.float32(1.0)
            else:
                k = 0 if dy > 0 else 1
                left, right = vert[k, 0], vert[k, 1]
                inside = jnp.where(gy + dy >= 0, 1.0, 0.0) * jnp.where(gy + dy < 16, 1.0, 0.0)
            west = unpack(side[AROUND.index((1, -dy))], 32) * jnp.where(gx > 0, 1.0, 0.0)
            east = unpack(side[AROUND.index((-1, -dy))], 64) * jnp.where(gx < 7, 1.0, 0.0)
            left, right = lane_roll(left, 64), lane_roll(right, 64)
            first = jnp.where(lane32 < 32, 0.0, jnp.where(lane32 < 64, west, left))
            middle = jnp.where(lane32 < 64, left, right)
            last = jnp.where(lane32 < 64, right, jnp.where(lane32 < 96, east, 0.0))
            bands.append(jnp.concatenate([first, middle, last], axis=1) * inside)
        return jnp.concatenate(bands, axis=0)

    packed_scaled[0] = pack(scaled_own[0], 0)
    packed_scaled[1] = pack(scaled_own[1], 96)
    scaled_copies = halo_copies(scaled_own, packed_scaled, vert_scaled, side_scaled, h_send, h_recv)
    for c in scaled_copies:
        c.start()

    for o in range(1, A_SIZE):
        id_copies[o].wait()
    spot = lax.broadcasted_iota(jnp.int32, (2 * B_SIZE, BX), 0)
    spot_lane = lax.broadcasted_iota(jnp.int32, (2 * B_SIZE, BX), 1)
    spot_p = spot // 2
    spot_y = (my_y + spot_p // NZ_CHIPS) % NY_CHIPS
    spot_z = (my_z + spot_p % NZ_CHIPS) % NZ_CHIPS
    owner = (my_x * 2 + spot_z // 2) * 16 + spot_y * 4 + (spot_z % 2) * 2 + my_c
    target = owner * 2 + spot % 2
    forward = jnp.zeros((2 * B_SIZE, BX), jnp.int32)
    for o in range(A_SIZE):
        ids = jnp.broadcast_to(idbuf[o, 0:1, :], (2 * B_SIZE, BX))
        hit = ids == target
        forward = forward + jnp.where(hit, spot_lane + (1 + SLOTS * o), 0)
        back = jnp.sum(jnp.where(hit, spot + 1, 0), axis=0, keepdims=True)
        back_vec[o : o + 1, :] = back
    forward_vec[...] = jnp.broadcast_to(jnp.sum(forward, axis=1, keepdims=True), forward.shape)
    to_scalar = [
        pltpu.make_async_copy(forward_vec, forward_idx, local_sem.at[0]),
        pltpu.make_async_copy(back_vec, back_idx, local_sem.at[1]),
    ]
    for c in to_scalar:
        c.start()
    for c in to_scalar:
        c.wait()

    for c in scaled_copies:
        c.wait()
    scaled_ext[...] = extended(scaled_own, vert_scaled, side_scaled)
    all_scaled = scaled_ext[...]
    east_w[...] = jnp.sqrt(all_scaled * lane_roll(all_scaled, -1))
    north_w[...] = jnp.sqrt(all_scaled * pltpu.roll(all_scaled, all_scaled.shape[0] - 1, 0))

    for o in range(1, A_SIZE):
        a_copies[o].wait()
    b_copies = [None] * B_SIZE
    for p in range(B_SIZE):
        for h in range(2):
            spread[p, h] = cand[jnp.clip(forward_idx[2 * p + h, 0], 0, SLOTS * A_SIZE)]
        if p > 0:
            b_copies[p] = copy(spread.at[p], gathered.at[p], b_send.at[p], b_recv.at[p], b_peer(p, 1))
            b_copies[p].start()
    for p in range(1, B_SIZE):
        b_copies[p].wait()
    for h in range(2):
        total = spread[0, h]
        for p in range(1, B_SIZE):
            total = total + gathered[p, h]
        source_own[h] = total * wet[:, h * BX : (h + 1) * BX]

    packed_source[0] = pack(source_own[0], 0)
    packed_source[1] = pack(source_own[1], 96)
    source_copies = halo_copies(source_own, packed_source, vert_source, side_source, g_send, g_recv)
    for c in source_copies:
        c.start()
    for c in source_copies:
        c.wait()
    start = extended(source_own, vert_source, side_source)
    centre, _ = chebyshev_table(STEPS)
    residual[...] = start
    direction[...] = start / centre
    height[...] = jnp.zeros_like(start)
    tall = start.shape[0]

    def advance(step, carry):
        now = direction[...]
        east_flux = east_w[...] * (now - lane_roll(now, -1))
        north_flux = north_w[...] * (now - pltpu.roll(now, tall - 1, 0))
        image = surface_shift * now + east_flux - lane_roll(east_flux, 1)
        image = image + north_flux - pltpu.roll(north_flux, 1, 0)
        height[...] = height[...] + now
        left = residual[...] - image
        residual[...] = left
        direction[...] = table_ref[2 * step] * now + table_ref[2 * step + 1] * left
        return carry

    lax.fori_loop(0, STEPS, advance, 0)

    def own_blocks(values):
        a, b, c = (lane_roll(values[:, k * BX : (k + 1) * BX], 64) for k in range(3))
        low = lax.broadcasted_iota(jnp.int32, a.shape, 1) < 64
        return jnp.where(low, a, b), jnp.where(low, b, c)

    mid = height[BY : 2 * BY, :]
    east_step = lane_roll(mid, -1) - mid
    north_step = height[BY + 1 : 2 * BY + 1, :] - mid
    south_step = mid - height[BY - 1 : 2 * BY - 1, :]
    east_energy = east_w[BY : 2 * BY, :] * east_step * east_step
    total = (
        east_energy
        + lane_roll(east_energy, 1)
        + north_w[BY : 2 * BY, :] * north_step * north_step
        + north_w[BY - 1 : 2 * BY - 1, :] * south_step * south_step
    )
    sens = 0.25 * total / jnp.maximum(scaled_ext[BY : 2 * BY, :], 0.25)
    sens_ref[:, :BX], sens_ref[:, BX:] = own_blocks(sens)
    own_heights = own_blocks(mid)
    surface_ref[:, :BX], surface_ref[:, BX:] = own_heights
    next_rows = own_blocks(height[2 * BY : 2 * BY + 8, :])
    row8 = lax.broadcasted_iota(jnp.int32, (8, BX), 0)
    for h in range(2):
        tile = mid[:, (h + 1) * BX : (h + 2) * BX]
        column = jnp.sum(jnp.where(lane32 == 64, tile, 0.0), axis=1, keepdims=True)
        flat = jnp.sum(jnp.where(row32 == lane32, column, 0.0), axis=0, keepdims=True)
        edge = jnp.where(row8 == 0, next_rows[h], jnp.where(row8 == 1, flat, 0.0))
        returned[1 + h, 0:BY, :] = own_heights[h]
        returned[1 + h, BY : BY + 8, :] = edge

    rb_copies = [None] * B_SIZE
    for p in range(1, B_SIZE):
        rb_copies[p] = copy(
            returned.at[pl.ds(1, 2)],
            returned.at[pl.ds(1 + 2 * p, 2)],
            rb_send.at[p],
            rb_recv.at[p],
            b_peer(p, -1),
        )
        rb_copies[p].start()
    for p in range(1, B_SIZE):
        rb_copies[p].wait()
    ra_copies = [None] * A_SIZE
    for o in range(A_SIZE):
        for s in range(SLOTS):
            slot_out[o, s] = returned[jnp.clip(back_idx[o, s], 0, 2 * B_SIZE)]
        if o > 0:
            ra_copies[o] = copy(slot_out.at[o], slot_in.at[o], ra_send.at[o], ra_recv.at[o], a_peer(o, -1))
            ra_copies[o].start()
    for o in range(1, A_SIZE):
        ra_copies[o].wait()
    for s in range(SLOTS):
        total = slot_out[0, s]
        for o in range(1, A_SIZE):
            total = total + slot_in[o, s]
        slot_sum[s] = total
        here = slot_sum[s, 0:BY, :]
        flat = jnp.broadcast_to(slot_sum[s, BY + 1 : BY + 2, :], (BY, BX))
        column = jnp.sum(jnp.where(row32 == lane32, flat, 0.0), axis=1, keepdims=True)
        beside = jnp.where(lane32 == BX - 1, column, lane_roll(here, -1))
        grads_ref[s, 0] = beside - here
        grads_ref[s, 1] = slot_sum[s, 1 : BY + 1, :] - here


def surface_solve(block_ids, forcing, bathymetry, land_mask):
    _, table = chebyshev_table(STEPS)
    flat_table = jnp.array([v for pair in table for v in pair], jnp.float32)
    f32, i32 = jnp.float32, jnp.int32
    wide = (3 * BY, 3 * BX)
    dma = pltpu.SemaphoreType.DMA
    vmem = pl.BlockSpec(memory_space=pltpu.VMEM)
    smem = pl.BlockSpec(memory_space=pltpu.SMEM)
    return pl.pallas_call(
        surface_kernel,
        out_shape=(
            jax.ShapeDtypeStruct((SLOTS, 2, BY, BX), f32),
            jax.ShapeDtypeStruct((BY, 2 * BX), f32),
            jax.ShapeDtypeStruct((BY, 2 * BX), f32),
        ),
        in_specs=[smem, smem, vmem, vmem, vmem],
        out_specs=(vmem, vmem, vmem),
        scratch_shapes=[
            pltpu.VMEM((A_SIZE, 8, BX), i32),
            pltpu.VMEM((2 * B_SIZE, BX), i32),
            pltpu.VMEM((A_SIZE, BX), i32),
            pltpu.SMEM((2 * B_SIZE, BX), i32),
            pltpu.SMEM((A_SIZE, BX), i32),
            pltpu.VMEM((1 + SLOTS * A_SIZE, BY, BX), f32),
            pltpu.VMEM((B_SIZE, 2, BY, BX), f32),
            pltpu.VMEM((B_SIZE, 2, BY, BX), f32),
            pltpu.VMEM((2, BY, BX), f32),
            pltpu.VMEM((2, BY, BX), f32),
            pltpu.VMEM((2, 8, BX), f32),
            pltpu.VMEM((2, 8, BX), f32),
            pltpu.VMEM((2, 2, BY, BX), f32),
            pltpu.VMEM((2, 2, BY, BX), f32),
            pltpu.VMEM((8, 8, BX), f32),
            pltpu.VMEM((8, 8, BX), f32),
            pltpu.VMEM(wide, f32),
            pltpu.VMEM(wide, f32),
            pltpu.VMEM(wide, f32),
            pltpu.VMEM(wide, f32),
            pltpu.VMEM(wide, f32),
            pltpu.VMEM(wide, f32),
            pltpu.VMEM((2, BY, BX), f32),
            pltpu.VMEM((1 + 2 * B_SIZE, HEIGHT_ROWS, BX), f32),
            pltpu.VMEM((A_SIZE, SLOTS, HEIGHT_ROWS, BX), f32),
            pltpu.VMEM((A_SIZE, SLOTS, HEIGHT_ROWS, BX), f32),
            pltpu.VMEM((SLOTS, HEIGHT_ROWS, BX), f32),
        ]
        + [dma((A_SIZE,))] * 4
        + [dma((B_SIZE,))] * 2
        + [dma((8,))] * 4
        + [dma((B_SIZE,))] * 2
        + [dma((A_SIZE,))] * 2
        + [dma((2,))],
        compiler_params=pltpu.CompilerParams(collective_id=0, has_side_effects=True),
        name="surface_solve",
    )(block_ids, flat_table, forcing, bathymetry, land_mask)


COL_ROWS = 16


def column_kernel(ids_ref, levels_ref, drag_ref, grads_ref, adjoint_ref, velocity_ref, out_ref, drag_out_ref):
    slot = pl.program_id(0)
    used = jnp.where(ids_ref[slot] < 256, 1.0, 0.0)
    tile = (COL_ROWS, BX)
    levels = levels_ref[0]
    zero = jnp.zeros(tile, jnp.float32)

    def masked(c, k):
        return jnp.where(levels > k, adjoint_ref[0, c, k], 0.0)

    flow_b = [zero, zero]
    column_b = [zero, zero]
    above0 = [masked(c, 0) for c in range(2)]
    flux0 = [zero, zero]
    above1 = [None, None]
    flux1 = [zero, zero]
    rate_prev = None
    for k in range(LEV + 1):
        if k < LEV - 1:
            rate_next = jnp.where(levels > k + 1, mix_rate, 0.0)
        bottom = levels == k
        for c in range(2):
            if k < LEV:
                if k < LEV - 1:
                    below = masked(c, k + 1)
                    flux = (below - above0[c]) * rate_next
                else:
                    below, flux = None, zero
                first = above0[c] + flux - flux0[c]
                flux0[c], above0[c] = flux, below
            if k > 0:
                if k < LEV:
                    flux = (first - above1[c]) * rate_prev
                else:
                    flux = zero
                second = above1[c] + flux - flux1[c]
                flux1[c] = flux
                out_ref[0, c, k - 1] = second
                column_b[c] = jnp.where(bottom, second, column_b[c])
                flow_b[c] = jnp.where(bottom, velocity_ref[0, c, k - 1].astype(jnp.float32), flow_b[c])
            above1[c] = first
        rate_prev = rate_next
    speed = jnp.sqrt(flow_b[0] * flow_b[0] + flow_b[1] * flow_b[1] + speed_floor)
    along = flow_b[0] * column_b[0] + flow_b[1] * column_b[1]
    ratio = along / speed
    drag = drag_ref[0]
    drag_out_ref[0] = -drag_step * speed * along * used
    for c in range(2):
        pull = drag_step * (drag * (speed * column_b[c] + flow_b[c] * ratio)) * used
        press = pressure_gain * grads_ref[0, c] * used
        for k in range(LEV):
            value = out_ref[0, c, k] * used
            value = value - jnp.where(levels == k + 1, pull, 0.0)
            out_ref[0, c, k] = value - jnp.where(levels > k, press, 0.0)


def columns(block_ids, level_count, drag_coef, grads, adjoint_vel, velocity):
    flat = pl.BlockSpec((1, COL_ROWS, BX), lambda s, r: (s, r, 0))
    deep = pl.BlockSpec((1, 2, LEV, COL_ROWS, BX), lambda s, r: (s, 0, 0, r, 0))
    return pl.pallas_call(
        column_kernel,
        grid=(SLOTS, BY // COL_ROWS),
        in_specs=[
            pl.BlockSpec(memory_space=pltpu.SMEM),
            flat,
            flat,
            pl.BlockSpec((1, 2, COL_ROWS, BX), lambda s, r: (s, 0, r, 0)),
            deep,
            deep,
        ],
        out_specs=(deep, flat),
        out_shape=(
            jax.ShapeDtypeStruct((SLOTS, 2, LEV, BY, BX), jnp.float32),
            jax.ShapeDtypeStruct((SLOTS, BY, BX), jnp.float32),
        ),
        name="columns",
    )(block_ids, level_count, drag_coef, grads, adjoint_vel, velocity)


def per_device(adjoint_vel, velocity, drag_coef, level_count, block_ids, bathymetry, land_mask):
    forcing = column_forcing(level_count, adjoint_vel)
    grads, surface, sens = surface_solve(block_ids, forcing, bathymetry, land_mask)
    corrected, drag_grad = columns(block_ids, level_count, drag_coef, grads, adjoint_vel, velocity)
    return (corrected, drag_grad, surface, sens)


def solution(mesh):
    slots = P(("gx", "gy"), None, None, None, None)
    flat = P(("gx", "gy"), None, None)
    return jax.shard_map(
        per_device,
        mesh=mesh,
        in_specs=(slots, slots, flat, flat, P(("gx", "gy")), P("gy", "gx"), P("gy", "gx")),
        out_specs=(slots, flat, P("gy", "gx"), P("gy", "gx")),
        check_vma=False,
    )
```

time: 1150 us -> 81.5 us (0.07)
  starting transfers between devices: 464 us -> 0 us
  waiting for transfers between devices: 402 us -> 0 us
  other arithmetic: 126 us -> 0 us
  Pallas kernels: 0 us -> 79.3 us
  blocking collectives: 68.7 us -> 0 us
  local copies, waits for them, and re-layouts: 46.9 us -> 1.24 us
  matrix products: 21 us -> 0 us
  between operations: 14.4 us -> 0.66 us
    ppermute x136 -> x0, starting transfers between devices: 464 us -> none  [the longest x68 351 us: padded(): lax.ppermute(tail, axis, [(i, (i + 1) % count) for i in range(ends)])]
    all_gather x2 -> x0, waiting for transfers between devices: 302 us -> none  [the longest x1 166 us: per_device(): piece = lax.all_gather(even_grads, ('gx', 'gy'), axis=0, tiled=True)]
    ppermute x136 -> x0, waiting for transfers between devices: 99.6 us -> none  [the longest x68 72.6 us: padded(): lax.ppermute(head, axis, [((i + 1) % count, i) for i in range(ends)])]
    pallas_call x0 -> x3, Pallas kernels: none -> 79.3 us  [the longest x1 62.2 us: surface_solve(): pl.pallas_call(surface_kernel, out_shape=(jax.ShapeDtypeStruct((SLOTS, 2,...]
    unnamed x1 -> x0, blocking collectives: 68.7 us -> none
    add x33 -> x0, other arithmetic: 45.2 us -> none  [the longest x32 45.2 us: advance(): coefs[step_index, 0] * direction + coefs[step_index, 1] * residual]
    dynamic_slice x32 -> x0, local copies, waits for them, and re-layouts: 43.3 us -> none  [advance(): coefs[step_index, 0] * direction + coefs[step_index, 1] * residual]
    mul x75 -> x0, other arithmetic: 41.8 us -> none  [the longest x3 16.8 us: column_block(): mix_rate * (column_field[:, 1:] - column_field[:, :-1]) * wet_below]
  transfers between devices with their start and end apart: 138 -> 0, of which waited for: 70 -> 0; matrix products, arithmetic and copies ran while one was open for 8% -> 0% of each run, Pallas kernels for 0% -> 0%
where the time goes in v1:
time: 81.5 us; the launch traced here: 81.2 us
  Pallas kernels  79.3 us (97%)
  local copies, waits for them, and re-layouts  1.24 us (2%)
    pallas_call x1, Pallas kernels, surface_solve(): pl.pallas_call(surface_kernel, out_shape=(jax.ShapeDtypeStruct((SLOTS, 2,...  62.2 us
    pallas_call x1, Pallas kernels, columns(): pl.pallas_call(column_kernel, grid=(SLOTS, BY // COL_ROWS), in_specs=[pl....  12.2 us
    pallas_call x1, Pallas kernels, column_forcing(): pl.pallas_call(forcing_kernel, grid=(SLOTS,), in_specs=[pl.BlockSpec((1,...  4.9 us

profile of v1, /device:TPU:1, one launch (start us, length us, event | category | flops | bytes accessed | tf_op | source)
XLA Modules:
  0.0 81.2 jit_solution(10661464371714583181)
XLA Ops:
  0.6 4.9 %column_forcing.1.forcing_ref = f32[4,32,128]{2,1,0:T(8,128)} custom-call(s32[4,32,128]{2,1,0:T(8,128)} %levels_ref.3, f32[4,2,62,32,128]{4,3,2,1,0:T(8,128)} %adjoint_ref.3), custom_call_target="tpu_custom_call" | custom-call | tf_op jit(solution)/shard_map/column_forcing/pallas_call | solution.py:53
  5.5 62.2 %surface_solve.1 = (f32[4,2,32,128]{3,2,1,0:T(8,128)}, f32[32,256]{1,0:T(8,128)}, f32[32,256]{1,0:T(8,128)}) custom-call(s32[4]{0:T(128)} %ids_ref.3, f32[64]{0:T(128)} %constant.2.clone.table_ref, f32[4,32,128]{2,1,0:T(8,128)} %column_forcing.1.forcing_ref, f32[32,256]{1,0:T(8,128)} %bathymetry_ref.1, s32[32,256]{1,0:T(8,128)} %mask_ref.1), custom_call_target="tpu_custom_call" | custom-call | tf_op jit(solution)/shard_map/surface_solve/pallas_call | solution.py:388
  67.7 0.0 copy-start.1
  67.7 0.0 copy-start
  67.7 12.2 %columns.1 = (f32[4,2,62,32,128]{4,3,2,1,0:T(8,128)}, f32[4,32,128]{2,1,0:T(8,128)}) custom-call(s32[4]{0:T(128)} %ids_ref.3, s32[4,32,128]{2,1,0:T(8,128)} %levels_ref.3, f32[4,32,128]{2,1,0:T(8,128)} %drag_ref.1, f32[4,2,32,128]{3,2,1,0:T(8,128)} %get-tuple-element.9.grads_ref, f32[4,2,62,32,128]{4,3,2,1,0:T(8,128)} %adjoint_ref.3, ...), custom_call_target="tpu_custom_call" | custom-call | tf_op jit(solution)/shard_map/columns/pallas_call | solution.py:499
  79.9 0.0 copy-done.1
  79.9 0.6 copy.14
  80.6 0.0 copy-done
  80.6 0.6 copy.15
Async XLA Ops:
  67.7 12.3 %copy-start.1 = (f32[32,256]{1,0:T(8,128)S(1)}, f32[32,256]{1,0:T(8,128)}, u32[]{:S(2)}) copy-start(f32[32,256]{1,0:T(8,128)} %get-tuple-element.20) | copy-start | bytes 98308
  67.7 12.9 %copy-start = (f32[32,256]{1,0:T(8,128)S(1)}, f32[32,256]{1,0:T(8,128)}, u32[]{:S(2)}) copy-start(f32[32,256]{1,0:T(8,128)} %get-tuple-element.21) | copy-start | bytes 98308

commit v2 on v1

v2 whole, which is shorter than its diff:
```python
import jax
import jax.numpy as jnp
from jax import lax
from jax.experimental import pallas as pl
from jax.experimental.pallas import tpu as pltpu
from jax.sharding import PartitionSpec as P

MESH = pl.DeviceIdType.MESH
STEPS = 32
LEV = 62
BY = 32
BX = 128
SLOTS = 4
CHUNKS = 4
CH = BY // CHUNKS
NX_CHIPS, NY_CHIPS, NZ_CHIPS, CORES = 4, 4, 4, 2
A_SIZE = NX_CHIPS * CORES
B_SIZE = NY_CHIPS * NZ_CHIPS
AROUND = ((-1, -1), (-1, 0), (-1, 1), (0, -1), (0, 1), (1, -1), (1, 0), (1, 1))
UNIT = 16
UNITS = SLOTS * BY // UNIT

mix_rate = 0.25
drag_step = 0.5
force_scale = 0.25
pressure_gain = 0.5
surface_shift = 1.0 / 64.0
speed_floor = 0.01


def chebyshev_table(total_steps):
    highest = surface_shift + 8.0
    centre = 0.5 * (highest + surface_shift)
    radius = 0.5 * (highest - surface_shift)
    sigma_ratio = centre / radius
    ratio_prev = 1.0 / sigma_ratio
    table = []
    for _ in range(total_steps):
        ratio_next = 1.0 / (2.0 * sigma_ratio - ratio_prev)
        table.append((ratio_next * ratio_prev, 2.0 * ratio_next / radius))
        ratio_prev = ratio_next
    return (centre, table)


def lane_roll(values, shift):
    return pltpu.roll(values, shift % values.shape[-1], values.ndim - 1)


def mix_unit(unit, levels_ref, drag_ref, mixed_ref, velocity_ref, pull_ref, drag_out_ref):
    slot = lax.div(unit, BY // UNIT)
    rows = pl.ds(pl.multiple_of(lax.rem(unit, BY // UNIT) * UNIT, UNIT), UNIT)
    levels = levels_ref[slot, rows, :]
    zero = jnp.zeros((UNIT, BX), jnp.float32)

    def level(k, state, first_level=False):
        above0, flux0, above1, flux1, flow_b, column_b, rate = state
        if isinstance(k, int):
            under = min(k + 1, LEV - 1)
        else:
            under = jnp.minimum(k + 1, LEV - 1)
        wet_next = levels > k + 1
        rate_next = jnp.where(wet_next, mix_rate, 0.0)
        bottom = levels == k
        out = [[], [], [], [], [], []]
        for c in range(2):
            below = jnp.where(wet_next, mixed_ref[slot, c, under, rows, :], 0.0)
            down = (below - above0[c]) * rate_next
            first = above0[c] + down - flux0[c]
            if first_level:
                down1, flow, col = zero, flow_b[c], column_b[c]
            else:
                down1 = (first - above1[c]) * rate
                second = above1[c] + down1 - flux1[c]
                mixed_ref[slot, c, k - 1, rows, :] = second
                col = jnp.where(bottom, second, column_b[c])
                flow = jnp.where(bottom, velocity_ref[slot, c, k - 1, rows, :].astype(jnp.float32), flow_b[c])
            for pile, value in zip(out, (below, down, first, down1, flow, col)):
                pile.append(value)
        return (*(tuple(pile) for pile in out), rate_next)

    wet_top = levels > 0
    top = tuple(jnp.where(wet_top, mixed_ref[slot, c, 0, rows, :], 0.0) for c in range(2))
    both = (zero, zero)
    state = (top, both, both, both, both, both, zero)
    state = level(0, state, first_level=True)
    state = level(1, state)
    state = level(2, state)

    def ten(j, state):
        for i in range(10):
            state = level(j * 10 + (3 + i), state)
        return state

    state = lax.fori_loop(0, (LEV - 2) // 10, ten, state)
    flow_b, column_b = state[4], state[5]
    speed = jnp.sqrt(flow_b[0] * flow_b[0] + flow_b[1] * flow_b[1] + speed_floor)
    along = flow_b[0] * column_b[0] + flow_b[1] * column_b[1]
    ratio = along / speed
    drag = drag_ref[slot, rows, :]
    drag_out_ref[slot, rows, :] = -drag_step * speed * along
    for c in range(2):
        pull_ref[slot, c, rows, :] = drag_step * (drag * (speed * column_b[c] + flow_b[c] * ratio))


def main_kernel(
    ids_ref,
    table_ref,
    count_ref,
    drag_ref,
    bathymetry_ref,
    mask_ref,
    adjoint_hbm,
    velocity_hbm,
    mixed_ref,
    press_ref,
    pull_ref,
    drag_out_ref,
    surface_ref,
    sens_ref,
    levels_ref,
    velocity_ref,
    idbuf,
    forward_vec,
    back_vec,
    forward_idx,
    back_idx,
    cand,
    spread,
    gathered,
    source_own,
    scaled_own,
    packed_scaled,
    packed_source,
    vert_scaled,
    vert_source,
    side_scaled,
    side_source,
    east_w,
    north_w,
    scaled_ext,
    direction,
    residual,
    height,
    returned,
    edge_pairs,
    edges,
    slot_out,
    slot_in,
    edge_out,
    edge_in,
    slot_sum,
    load_sem,
    id_send,
    id_recv,
    a_send,
    a_recv,
    b_send,
    b_recv,
    h_send,
    h_recv,
    g_send,
    g_recv,
    rb_send,
    rb_recv,
    ra_send,
    ra_recv,
    local_sem,
):
    gx = lax.axis_index("gx")
    gy = lax.axis_index("gy")
    my_x, my_zh = lax.div(gx, 2), lax.rem(gx, 2)
    my_y, my_zl, my_c = lax.div(gy, 4), lax.rem(lax.div(gy, 2), 2), lax.rem(gy, 2)
    my_z = my_zh * 2 + my_zl

    def a_peer(o, sign):
        step_x, step_c = o // 2, o % 2
        if sign < 0:
            step_x = (NX_CHIPS - step_x) % NX_CHIPS
        x = lax.rem(my_x + step_x, NX_CHIPS)
        c = lax.rem(my_c + step_c, CORES)
        return (x * 2 + my_zh, my_y * 4 + my_zl * 2 + c)

    def b_peer(p, sign):
        step_y, step_z = p // NZ_CHIPS, p % NZ_CHIPS
        if sign < 0:
            step_y = (NY_CHIPS - step_y) % NY_CHIPS
            step_z = (NZ_CHIPS - step_z) % NZ_CHIPS
        y = lax.rem(my_y + step_y, NY_CHIPS)
        z = lax.rem(my_z + step_z, NZ_CHIPS)
        return (my_x * 2 + lax.div(z, 2), y * 4 + lax.rem(z, 2) * 2 + my_c)

    def near(n):
        dx, dy = AROUND[n]
        return (lax.rem(gx + dx + 8, 8), lax.rem(gy + dy + 16, 16))

    def copy(src, dst, send, recv, to):
        return pltpu.make_async_remote_copy(
            src_ref=src, dst_ref=dst, send_sem=send, recv_sem=recv, device_id=to, device_id_type=MESH
        )

    a_order = sorted(range(1, A_SIZE), key=lambda o: -min(o // 2, NX_CHIPS - o // 2))
    b_order = sorted(
        range(1, B_SIZE),
        key=lambda p: -min(p // NZ_CHIPS, NY_CHIPS - p // NZ_CHIPS) - min(p % NZ_CHIPS, NZ_CHIPS - p % NZ_CHIPS),
    )

    loads = []
    for q in range(CHUNKS):
        part = (slice(None), slice(None), slice(None), pl.ds(q * CH, CH))
        loads.append(pltpu.make_async_copy(adjoint_hbm.at[part], mixed_ref.at[part], load_sem.at[q]))
    loads.append(pltpu.make_async_copy(velocity_hbm, velocity_ref, load_sem.at[CHUNKS]))
    for c in loads:
        c.start()

    barrier = pltpu.get_barrier_semaphore()
    for o in range(1, A_SIZE):
        pl.semaphore_signal(barrier, inc=1, device_id=a_peer(o, 1), device_id_type=MESH)
    for p in range(1, B_SIZE):
        pl.semaphore_signal(barrier, inc=1, device_id=b_peer(p, 1), device_id_type=MESH)
    for n in range(8):
        pl.semaphore_signal(barrier, inc=1, device_id=near(n), device_id_type=MESH)

    lane8 = lax.broadcasted_iota(jnp.int32, (8, BX), 1)
    lane32 = lax.broadcasted_iota(jnp.int32, (BY, BX), 1)
    row8 = lax.broadcasted_iota(jnp.int32, (8, BX), 0)
    row32 = lax.broadcasted_iota(jnp.int32, (BY, BX), 0)

    id_row = jnp.full((8, BX), -1, jnp.int32)
    for s in range(SLOTS):
        id_row = jnp.where(lane8 == s, ids_ref[s], id_row)
        levels_ref[s] = count_ref[s] * jnp.where(ids_ref[s] < 256, 1, 0)
    idbuf[0] = id_row
    for q in range(CHUNKS):
        cand[q][0] = jnp.zeros((CH, BX), jnp.float32)
        returned[q][0] = jnp.zeros((CH, BX), jnp.float32)
    edges[0] = jnp.zeros((8, BX), jnp.float32)

    def pack(block, base):
        out = jnp.zeros((8, BX), jnp.float32)
        for q in range(4):
            part = lane_roll(block[8 * q : 8 * q + 8, :], 32 * q - base)
            out = jnp.where(lane8 // 32 == q, part, out)
        return out

    def unpack(packed, base):
        return jnp.concatenate([lane_roll(packed, base - 32 * q) for q in range(4)], axis=0)

    wet = mask_ref[...].astype(jnp.float32)
    scaled = bathymetry_ref[...] * wet
    scaled_own[0] = scaled[:, :BX]
    scaled_own[1] = scaled[:, BX:]
    packed_scaled[0] = pack(scaled_own[0], 0)
    packed_scaled[1] = pack(scaled_own[1], 96)

    def force(q):
        rows = slice(q * CH, (q + 1) * CH)

        def one(s, carry):
            levels = levels_ref[s, rows, :]
            totals = [jnp.zeros((CH, BX), jnp.float32)] * 4
            for k in range(LEV):
                pair = mixed_ref[s, 0, k, rows, :] + mixed_ref[s, 1, k, rows, :]
                totals[k % 4] = totals[k % 4] + jnp.where(levels > k, pair, 0.0)
            cand[q][1 + s] = force_scale * ((totals[0] + totals[1]) + (totals[2] + totals[3]))
            return carry

        lax.fori_loop(0, SLOTS, one, 0)

    loads[0].wait()
    force(0)
    pl.semaphore_wait(barrier, A_SIZE - 1 + B_SIZE - 1 + 8)

    id_copies = {}
    for o in a_order:
        id_copies[o] = copy(idbuf.at[0], idbuf.at[o], id_send.at[o], id_recv.at[o], a_peer(o, 1))
        id_copies[o].start()

    a_copies = [{} for _ in range(CHUNKS)]

    def send_a(q):
        for o in a_order:
            a_copies[q][o] = copy(
                cand[q].at[pl.ds(1, SLOTS)],
                cand[q].at[pl.ds(1 + SLOTS * o, SLOTS)],
                a_send.at[q, o],
                a_recv.at[q, o],
                a_peer(o, 1),
            )
            a_copies[q][o].start()

    send_a(0)

    def halo_copies(own, packed, vert, side, send, recv):
        copies = []
        for n, (dx, dy) in enumerate(AROUND):
            if dx == 0:
                src, dst = own, vert.at[0 if dy < 0 else 1]
            else:
                src, dst = packed.at[0 if dx < 0 else 1], side.at[n]
            copies.append(copy(src, dst, send.at[n], recv.at[n], near(n)))
        return copies

    def extended(own, vert, side):
        bands = []
        for dy in (-1, 0, 1):
            if dy == 0:
                left, right = own[0], own[1]
                inside = jnp.float32(1.0)
            else:
                k = 0 if dy > 0 else 1
                left, right = vert[k, 0], vert[k, 1]
                inside = jnp.where(gy + dy >= 0, 1.0, 0.0) * jnp.where(gy + dy < 16, 1.0, 0.0)
            west = unpack(side[AROUND.index((1, -dy))], 32) * jnp.where(gx > 0, 1.0, 0.0)
            east = unpack(side[AROUND.index((-1, -dy))], 64) * jnp.where(gx < 7, 1.0, 0.0)
            left, right = lane_roll(left, 64), lane_roll(right, 64)
            first = jnp.where(lane32 < 32, 0.0, jnp.where(lane32 < 64, west, left))
            middle = jnp.where(lane32 < 64, left, right)
            last = jnp.where(lane32 < 64, right, jnp.where(lane32 < 96, east, 0.0))
            bands.append(jnp.concatenate([first, middle, last], axis=1) * inside)
        return jnp.concatenate(bands, axis=0)

    for q in range(1, CHUNKS):
        loads[q].wait()
        force(q)
        send_a(q)

    scaled_copies = halo_copies(scaled_own, packed_scaled, vert_scaled, side_scaled, h_send, h_recv)
    for c in scaled_copies:
        c.start()

    for o in a_order:
        id_copies[o].wait()
    spot = lax.broadcasted_iota(jnp.int32, (2 * B_SIZE, BX), 0)
    spot_lane = lax.broadcasted_iota(jnp.int32, (2 * B_SIZE, BX), 1)
    spot_p = spot // 2
    spot_y = (my_y + spot_p // NZ_CHIPS) % NY_CHIPS
    spot_z = (my_z + spot_p % NZ_CHIPS) % NZ_CHIPS
    owner = (my_x * 2 + spot_z // 2) * 16 + spot_y * 4 + (spot_z % 2) * 2 + my_c
    target = owner * 2 + spot % 2
    forward = jnp.zeros((2 * B_SIZE, BX), jnp.int32)
    for o in range(A_SIZE):
        ids = jnp.broadcast_to(idbuf[o, 0:1, :], (2 * B_SIZE, BX))
        hit = ids == target
        forward = forward + jnp.where(hit, spot_lane + (1 + SLOTS * o), 0)
        back = jnp.sum(jnp.where(hit, spot + 1, 0), axis=0, keepdims=True)
        back_vec[o : o + 1, :] = back
    forward_vec[...] = jnp.broadcast_to(jnp.sum(forward, axis=1, keepdims=True), forward.shape)
    to_scalar = [
        pltpu.make_async_copy(forward_vec, forward_idx, local_sem.at[0]),
        pltpu.make_async_copy(back_vec, back_idx, local_sem.at[1]),
    ]
    for c in to_scalar:
        c.start()
    for c in to_scalar:
        c.wait()

    def picked(r):
        return jnp.clip(forward_idx[r, 0], 0, SLOTS * A_SIZE)

    def back_of(o, s):
        return jnp.clip(back_idx[o, s], 0, 2 * B_SIZE)

    def units(first, last):
        def one(unit, carry):
            mix_unit(unit, levels_ref, drag_ref, mixed_ref, velocity_ref, pull_ref, drag_out_ref)
            return carry

        lax.fori_loop(first, last, one, 0)

    loads[CHUNKS].wait()
    b_copies = [{} for _ in range(CHUNKS)]
    for q in range(CHUNKS):
        for o in a_order:
            a_copies[q][o].wait()
        for p in b_order + [0]:
            for h in range(2):
                spread[q, p, h] = cand[q][picked(2 * p + h)]
            if p > 0:
                b_copies[q][p] = copy(
                    spread.at[q, p], gathered.at[q, p], b_send.at[q, p], b_recv.at[q, p], b_peer(p, 1)
                )
                b_copies[q][p].start()

    units(0, UNITS)
    for c in scaled_copies:
        c.wait()
    scaled_ext[...] = extended(scaled_own, vert_scaled, side_scaled)
    all_scaled = scaled_ext[...]
    tall = all_scaled.shape[0]
    east_w[...] = jnp.sqrt(all_scaled * lane_roll(all_scaled, -1))
    north_w[...] = jnp.sqrt(all_scaled * pltpu.roll(all_scaled, tall - 1, 0))

    for q in range(CHUNKS):
        for p in b_order:
            b_copies[q][p].wait()
        rows = slice(q * CH, (q + 1) * CH)
        for h in range(2):
            total = spread[q, 0, h]
            for p in range(1, B_SIZE):
                total = total + gathered[q, p, h]
            source_own[h, rows, :] = total * wet[rows, h * BX : (h + 1) * BX]

    packed_source[0] = pack(source_own[0], 0)
    packed_source[1] = pack(source_own[1], 96)
    source_copies = halo_copies(source_own, packed_source, vert_source, side_source, g_send, g_recv)
    for c in source_copies:
        c.start()
    for c in source_copies:
        c.wait()
    start = extended(source_own, vert_source, side_source)
    centre, _ = chebyshev_table(STEPS)
    residual[...] = start
    direction[...] = start / centre
    core = slice(BY - 8, 2 * BY + 8)
    height[...] = jnp.zeros(height.shape, jnp.float32)

    for phase in range(4):
        band = slice(8 * phase, tall - 8 * phase)
        wide = tall - 16 * phase

        def advance(step, carry, band=band, wide=wide, phase=phase):
            now = direction[band, :]
            inner = slice(BY - 8 - 8 * phase, BY - 8 - 8 * phase + BY + 16)
            height[...] = height[...] + now[inner, :]
            east_flux = east_w[band, :] * (now - lane_roll(now, -1))
            north_flux = north_w[band, :] * (now - pltpu.roll(now, wide - 1, 0))
            image = surface_shift * now + east_flux - lane_roll(east_flux, 1)
            image = image + north_flux - pltpu.roll(north_flux, 1, 0)
            left = residual[band, :] - image
            residual[band, :] = left
            direction[band, :] = table_ref[2 * step] * now + table_ref[2 * step + 1] * left
            return carry

        lax.fori_loop(8 * phase, min(8 * phase + 8, STEPS - 1), advance, 0)
    height[...] = height[...] + direction[core, :]

    def own_blocks(values):
        a, b, c = (lane_roll(values[:, k * BX : (k + 1) * BX], 64) for k in range(3))
        low = lax.broadcasted_iota(jnp.int32, a.shape, 1) < 64
        return jnp.where(low, a, b), jnp.where(low, b, c)

    mid = height[8 : BY + 8, :]
    own_heights = own_blocks(mid)
    next_rows = own_blocks(height[BY + 8 : BY + 16, :])
    pair = jnp.zeros((8, BX), jnp.float32)
    for h in range(2):
        tile = mid[:, (h + 1) * BX : (h + 2) * BX]
        column = jnp.sum(jnp.where(lane32 == 64, tile, 0.0), axis=1, keepdims=True)
        flat = jnp.sum(jnp.where(row32 == lane32, column, 0.0), axis=0, keepdims=True)
        next_row = next_rows[h] if h == 0 else pltpu.roll(next_rows[h], 2 * h, 0)
        pair = jnp.where(row8 == 2 * h, next_row, jnp.where(row8 == 2 * h + 1, flat, pair))
        for q in range(CHUNKS):
            returned[q][1 + h] = own_heights[h][q * CH : (q + 1) * CH, :]
    edge_pairs[0] = pair

    rb_copies = [{} for _ in range(CHUNKS + 1)]
    for p in b_order:
        rb_copies[CHUNKS][p] = copy(
            edge_pairs.at[0], edge_pairs.at[p], rb_send.at[CHUNKS, p], rb_recv.at[CHUNKS, p], b_peer(p, -1)
        )
        rb_copies[CHUNKS][p].start()
    for q in range(CHUNKS):
        for p in b_order:
            rb_copies[q][p] = copy(
                returned[q].at[pl.ds(1, 2)],
                returned[q].at[pl.ds(1 + 2 * p, 2)],
                rb_send.at[q, p],
                rb_recv.at[q, p],
                b_peer(p, -1),
            )
            rb_copies[q][p].start()

    east_step = lane_roll(mid, -1) - mid
    north_step = height[9 : BY + 9, :] - mid
    south_step = mid - height[7 : BY + 7, :]
    east_energy = east_w[BY : 2 * BY, :] * east_step * east_step
    total = (
        east_energy
        + lane_roll(east_energy, 1)
        + north_w[BY : 2 * BY, :] * north_step * north_step
        + north_w[BY - 1 : 2 * BY - 1, :] * south_step * south_step
    )
    sens = 0.25 * total / jnp.maximum(scaled_ext[BY : 2 * BY, :], 0.25)
    sens_ref[:, :BX], sens_ref[:, BX:] = own_blocks(sens)
    surface_ref[:, :BX], surface_ref[:, BX:] = own_heights

    ra_copies = [{} for _ in range(CHUNKS + 1)]
    for p in b_order:
        rb_copies[CHUNKS][p].wait()
    for p in range(B_SIZE):
        both = edge_pairs[p]
        edges[1 + 2 * p] = jnp.where(row8 < 2, both, 0.0)
        edges[2 + 2 * p] = jnp.where(row8 < 2, pltpu.roll(both, 6, 0), 0.0)
    for o in a_order + [0]:
        tile = edges[back_of(o, 0)]
        for s in range(1, SLOTS):
            tile = tile + pltpu.roll(edges[back_of(o, s)], 2 * s, 0)
        edge_out[o] = tile
        if o > 0:
            ra_copies[CHUNKS][o] = copy(
                edge_out.at[o], edge_in.at[o], ra_send.at[CHUNKS, o], ra_recv.at[CHUNKS, o], a_peer(o, -1)
            )
            ra_copies[CHUNKS][o].start()
    for q in range(CHUNKS):
        for p in b_order:
            rb_copies[q][p].wait()
        for o in a_order + [0]:
            for s in range(SLOTS):
                slot_out[q, o, s] = returned[q][back_of(o, s)]
            if o > 0:
                ra_copies[q][o] = copy(
                    slot_out.at[q, o], slot_in.at[q, o], ra_send.at[q, o], ra_recv.at[q, o], a_peer(o, -1)
                )
                ra_copies[q][o].start()
    for o in a_order:
        ra_copies[CHUNKS][o].wait()
    edge = edge_out[0]
    for o in range(1, A_SIZE):
        edge = edge + edge_in[o]
    for s in range(SLOTS):
        slot_sum[s, BY : BY + 8, :] = edge if s == 0 else pltpu.roll(edge, 8 - 2 * s, 0)
    for q in range(CHUNKS):
        for o in a_order:
            ra_copies[q][o].wait()
        for s in range(SLOTS):
            total = slot_out[q, 0, s]
            for o in range(1, A_SIZE):
                total = total + slot_in[q, o, s]
            slot_sum[s, q * CH : (q + 1) * CH, :] = total
    for s in range(SLOTS):
        here = slot_sum[s, 0:BY, :]
        flat = jnp.broadcast_to(slot_sum[s, BY + 1 : BY + 2, :], (BY, BX))
        column = jnp.sum(jnp.where(row32 == lane32, flat, 0.0), axis=1, keepdims=True)
        beside = jnp.where(lane32 == BX - 1, column, lane_roll(here, -1))
        press_ref[s, 0] = pressure_gain * (beside - here)
        press_ref[s, 1] = pressure_gain * (slot_sum[s, 1 : BY + 1, :] - here)


def main_call(block_ids, level_count, drag_coef, bathymetry, land_mask, adjoint_vel, velocity):
    _, table = chebyshev_table(STEPS)
    flat_table = jnp.array([v for pair in table for v in pair], jnp.float32)
    f32, i32 = jnp.float32, jnp.int32
    wide = (3 * BY, 3 * BX)
    dma = pltpu.SemaphoreType.DMA
    vmem = pl.BlockSpec(memory_space=pltpu.VMEM)
    smem = pl.BlockSpec(memory_space=pltpu.SMEM)
    hbm = pl.BlockSpec(memory_space=pltpu.HBM)
    return pl.pallas_call(
        main_kernel,
        out_shape=(
            pltpu.VMEM((SLOTS, 2, LEV, BY, BX), f32),
            pltpu.VMEM((SLOTS, 2, BY, BX), f32),
            pltpu.VMEM((SLOTS, 2, BY, BX), f32),
            pltpu.VMEM((SLOTS, BY, BX), f32),
            pltpu.VMEM((BY, 2 * BX), f32),
            pltpu.VMEM((BY, 2 * BX), f32),
        ),
        in_specs=[smem, smem, vmem, vmem, vmem, vmem, hbm, hbm],
        out_specs=(vmem,) * 6,
        scratch_shapes=[
            pltpu.VMEM((SLOTS, BY, BX), i32),
            pltpu.VMEM((SLOTS, 2, LEV, BY, BX), jnp.bfloat16),
            pltpu.VMEM((A_SIZE, 8, BX), i32),
            pltpu.VMEM((2 * B_SIZE, BX), i32),
            pltpu.VMEM((A_SIZE, BX), i32),
            pltpu.SMEM((2 * B_SIZE, BX), i32),
            pltpu.SMEM((A_SIZE, BX), i32),
            [pltpu.VMEM((1 + SLOTS * A_SIZE, CH, BX), f32) for _ in range(CHUNKS)],
            pltpu.VMEM((CHUNKS, B_SIZE, 2, CH, BX), f32),
            pltpu.VMEM((CHUNKS, B_SIZE, 2, CH, BX), f32),
            pltpu.VMEM((2, BY, BX), f32),
            pltpu.VMEM((2, BY, BX), f32),
            pltpu.VMEM((2, 8, BX), f32),
            pltpu.VMEM((2, 8, BX), f32),
            pltpu.VMEM((2, 2, BY, BX), f32),
            pltpu.VMEM((2, 2, BY, BX), f32),
            pltpu.VMEM((8, 8, BX), f32),
            pltpu.VMEM((8, 8, BX), f32),
            pltpu.VMEM(wide, f32),
            pltpu.VMEM(wide, f32),
            pltpu.VMEM(wide, f32),
            pltpu.VMEM(wide, f32),
            pltpu.VMEM(wide, f32),
            pltpu.VMEM((BY + 16, 3 * BX), f32),
            [pltpu.VMEM((1 + 2 * B_SIZE, CH, BX), f32) for _ in range(CHUNKS)],
            pltpu.VMEM((B_SIZE, 8, BX), f32),
            pltpu.VMEM((1 + 2 * B_SIZE, 8, BX), f32),
            pltpu.VMEM((CHUNKS, A_SIZE, SLOTS, CH, BX), f32),
            pltpu.VMEM((CHUNKS, A_SIZE, SLOTS, CH, BX), f32),
            pltpu.VMEM((A_SIZE, 8, BX), f32),
            pltpu.VMEM((A_SIZE, 8, BX), f32),
            pltpu.VMEM((SLOTS, BY + 8, BX), f32),
            dma((CHUNKS + 1,)),
            dma((A_SIZE,)),
            dma((A_SIZE,)),
            dma((CHUNKS, A_SIZE)),
            dma((CHUNKS, A_SIZE)),
            dma((CHUNKS, B_SIZE)),
            dma((CHUNKS, B_SIZE)),
            dma((8,)),
            dma((8,)),
            dma((8,)),
            dma((8,)),
            dma((CHUNKS + 1, B_SIZE)),
            dma((CHUNKS + 1, B_SIZE)),
            dma((CHUNKS + 1, A_SIZE)),
            dma((CHUNKS + 1, A_SIZE)),
            dma((2,)),
        ],
        compiler_params=pltpu.CompilerParams(
            collective_id=0, has_side_effects=True, vmem_limit_bytes=50 * 2**20
        ),
        name="columns_and_surface",
    )(block_ids, flat_table, level_count, drag_coef, bathymetry, land_mask, adjoint_vel, velocity)


def final_kernel(
    count_ref, mixed_ref, press_ref, pull_ref, drag_ref, surface_ref, sens_ref,
    out_hbm, drag_out_ref, surface_out_ref, sens_out_ref, stage, sems,
):
    drag_out_ref[...] = drag_ref[...]
    surface_out_ref[...] = surface_ref[...]
    sens_out_ref[...] = sens_ref[...]
    puts = []
    for unit in range(UNITS):
        slot, rows = unit // (BY // UNIT), slice(unit % (BY // UNIT) * UNIT, unit % (BY // UNIT) * UNIT + UNIT)
        levels = count_ref[slot, rows, :]
        press = [press_ref[slot, c, rows, :] for c in range(2)]
        bed = [press[c] + pull_ref[slot, c, rows, :] for c in range(2)]
        for k in range(LEV):
            wet, bottom = levels > k, levels == k + 1
            for c in range(2):
                less = jnp.where(bottom, bed[c], jnp.where(wet, press[c], 0.0))
                stage[slot, c, k, rows, :] = mixed_ref[slot, c, k, rows, :] - less
        part = (slot, slice(None), slice(None), pl.ds(unit % (BY // UNIT) * UNIT, UNIT))
        puts.append(pltpu.make_async_copy(stage.at[part], out_hbm.at[part], sems.at[unit]))
        puts[-1].start()
    for c in puts:
        c.wait()


def final_call(level_count, mixed, press, pull, drag_grad, surface, sens):
    f32 = jnp.float32
    vmem = pl.BlockSpec(memory_space=pltpu.VMEM)
    deep = (SLOTS, 2, LEV, BY, BX)
    return pl.pallas_call(
        final_kernel,
        out_shape=(
            jax.ShapeDtypeStruct(deep, f32),
            jax.ShapeDtypeStruct(drag_grad.shape, f32),
            jax.ShapeDtypeStruct(surface.shape, f32),
            jax.ShapeDtypeStruct(sens.shape, f32),
        ),
        in_specs=[vmem] * 7,
        out_specs=(pl.BlockSpec(memory_space=pltpu.HBM), vmem, vmem, vmem),
        scratch_shapes=[pltpu.VMEM(deep, f32), pltpu.SemaphoreType.DMA((UNITS,))],
        compiler_params=pltpu.CompilerParams(vmem_limit_bytes=24 * 2**20),
        name="pressure_correction",
    )(level_count, mixed, press, pull, drag_grad, surface, sens)


def per_device(adjoint_vel, velocity, drag_coef, level_count, block_ids, bathymetry, land_mask):
    mixed, press, pull, drag_grad, surface, sens = main_call(
        block_ids, level_count, drag_coef, bathymetry, land_mask, adjoint_vel, velocity
    )
    return final_call(level_count, mixed, press, pull, drag_grad, surface, sens)


def solution(mesh):
    slots = P(("gx", "gy"), None, None, None, None)
    flat = P(("gx", "gy"), None, None)
    return jax.shard_map(
        per_device,
        mesh=mesh,
        in_specs=(slots, slots, flat, flat, P(("gx", "gy")), P("gy", "gx"), P("gy", "gx")),
        out_specs=(slots, flat, P("gy", "gx"), P("gy", "gx")),
        check_vma=False,
    )
```

time: 81.5 us -> 63 us (0.77)
  Pallas kernels: 79.3 us -> 62.2 us
  local copies, waits for them, and re-layouts: 1.24 us -> 0.01 us
    pallas_call x3 -> x2, Pallas kernels: 79.3 us -> 62.2 us  [the longest x1 58.1 us: main_call(): pl.pallas_call(main_kernel, out_shape=(pltpu.VMEM((SLOTS, 2, LEV, BY, BX)...]
    unnamed x6 -> x2, local copies, waits for them, and re-layouts: 1.24 us -> 0.01 us
where the time goes in v2:
time: 63 us; the launch traced here: 62.9 us
  Pallas kernels  62.2 us (99%)
  between operations  0.66 us (1%)
    pallas_call x1, Pallas kernels, main_call(): pl.pallas_call(main_kernel, out_shape=(pltpu.VMEM((SLOTS, 2, LEV, BY, BX)...  58.1 us
    pallas_call x1, Pallas kernels, final_call(): pl.pallas_call(final_kernel, out_shape=(jax.ShapeDtypeStruct(deep, f32),...  4.09 us

profile of v2, /device:TPU:1, one launch (start us, length us, event | category | flops | bytes accessed | tf_op | source)
XLA Modules:
  0.0 62.9 jit_solution(4230764629483053427)
XLA Ops:
  0.6 0.0 copy-start
  0.6 58.1 %columns_and_surface.1 = (f32[4,2,62,32,128]{4,3,2,1,0:T(8,128)S(1)}, f32[4,2,32,128]{3,2,1,0:T(8,128)S(1)}, f32[4,2,32,128]{3,2,1,0:T(8,128)S(1)}, f32[4,32,128...) custom-call(s32[4]{0:T(128)} %ids_ref.1, f32[64]{0:T(128)} %constant.2.clone.table_ref, ...), custom_call_target="tpu_custom_call" | custom-call | tf_op jit(solution)/shard_map/columns_and_surface/pallas_call | solution.py:548
  58.8 0.0 copy-done
  58.8 4.1 %pressure_correction.1 = (f32[4,2,62,32,128]{4,3,2,1,0:T(8,128)}, f32[4,32,128]{2,1,0:T(8,128)}, f32[32,256]{1,0:T(8,128)}, f32[32,256]{1,0:T(8,128)}) custom-call(s32[4,32,128]{2,1,0:T(8,128)S(1)} %copy-done, f32[4,2,62,32,128]{4,3,2,1,0:T(8,128)S(1)} %get-tuple-element.10.mixed_ref, f32[4,2,32,128]{3,2,1,0:T(8,128)S(1)} %get-tuple-element.11.press_ref, ...), custom_call_target="tpu_custom_call" | custom-call | tf_op jit(solution)/shard_map/pressure_correction/pallas_call | solution.py:646
Async XLA Ops:
  0.6 58.2 %copy-start = (s32[4,32,128]{2,1,0:T(8,128)S(1)}, s32[4,32,128]{2,1,0:T(8,128)}, u32[]{:S(2)}) copy-start(s32[4,32,128]{2,1,0:T(8,128)} %count_ref.3) | copy-start | bytes 196612

commit v3 on v2

--- a/solution.py
+++ b/solution.py
@@ -54,22 +54,23 @@
 
     def level(k, state, first_level=False):
         above0, flux0, above1, flux1, flow_b, column_b, rate = state
-        if isinstance(k, int):
-            under = min(k + 1, LEV - 1)
-        else:
-            under = jnp.minimum(k + 1, LEV - 1)
+        last = k >= LEV - 1
         wet_next = levels > k + 1
         rate_next = jnp.where(wet_next, mix_rate, 0.0)
         bottom = levels == k
         out = [[], [], [], [], [], []]
         for c in range(2):
-            below = jnp.where(wet_next, mixed_ref[slot, c, under, rows, :], 0.0)
-            down = (below - above0[c]) * rate_next
-            first = above0[c] + down - flux0[c]
+            if last:
+                below = down = zero
+                first = above0[c] - flux0[c]
+            else:
+                below = jnp.where(wet_next, mixed_ref[slot, c, k + 1, rows, :], 0.0)
+                down = (below - above0[c]) * rate_next
+                first = above0[c] + down - flux0[c]
             if first_level:
                 down1, flow, col = zero, flow_b[c], column_b[c]
             else:
-                down1 = (first - above1[c]) * rate
+                down1 = zero if k == LEV else (first - above1[c]) * rate
                 second = above1[c] + down1 - flux1[c]
                 mixed_ref[slot, c, k - 1, rows, :] = second
                 col = jnp.where(bottom, second, column_b[c])
@@ -81,17 +82,9 @@
     wet_top = levels > 0
     top = tuple(jnp.where(wet_top, mixed_ref[slot, c, 0, rows, :], 0.0) for c in range(2))
     both = (zero, zero)
-    state = (top, both, both, both, both, both, zero)
-    state = level(0, state, first_level=True)
-    state = level(1, state)
-    state = level(2, state)
-
-    def ten(j, state):
-        for i in range(10):
-            state = level(j * 10 + (3 + i), state)
-        return state
-
-    state = lax.fori_loop(0, (LEV - 2) // 10, ten, state)
+    state = level(0, (top, both, both, both, both, both, zero), first_level=True)
+    for k in range(1, LEV + 1):
+        state = level(k, state)
     flow_b, column_b = state[4], state[5]
     speed = jnp.sqrt(flow_b[0] * flow_b[0] + flow_b[1] * flow_b[1] + speed_floor)
     along = flow_b[0] * column_b[0] + flow_b[1] * column_b[1]
@@ -141,6 +134,9 @@
     direction,
     residual,
     height,
+    west_w,
+    south_w,
+    diagonal,
     returned,
     edge_pairs,
     edges,
@@ -319,6 +315,13 @@
             bands.append(jnp.concatenate([first, middle, last], axis=1) * inside)
         return jnp.concatenate(bands, axis=0)
 
+    def units(first, last):
+        def one(unit, carry):
+            mix_unit(unit, levels_ref, drag_ref, mixed_ref, velocity_ref, pull_ref, drag_out_ref)
+            return carry
+
+        lax.fori_loop(first, last, one, 0)
+
     for q in range(1, CHUNKS):
         loads[q].wait()
         force(q)
@@ -328,6 +331,8 @@
     for c in scaled_copies:
         c.start()
 
+    loads[CHUNKS].wait()
+    units(0, 2)
     for o in a_order:
         id_copies[o].wait()
     spot = lax.broadcasted_iota(jnp.int32, (2 * B_SIZE, BX), 0)
@@ -360,14 +365,6 @@
     def back_of(o, s):
         return jnp.clip(back_idx[o, s], 0, 2 * B_SIZE)
 
-    def units(first, last):
-        def one(unit, carry):
-            mix_unit(unit, levels_ref, drag_ref, mixed_ref, velocity_ref, pull_ref, drag_out_ref)
-            return carry
-
-        lax.fori_loop(first, last, one, 0)
-
-    loads[CHUNKS].wait()
     b_copies = [{} for _ in range(CHUNKS)]
     for q in range(CHUNKS):
         for o in a_order:
@@ -381,7 +378,7 @@
                 )
                 b_copies[q][p].start()
 
-    units(0, UNITS)
+    units(2, 6)
     for c in scaled_copies:
         c.wait()
     scaled_ext[...] = extended(scaled_own, vert_scaled, side_scaled)
@@ -389,6 +386,9 @@
     tall = all_scaled.shape[0]
     east_w[...] = jnp.sqrt(all_scaled * lane_roll(all_scaled, -1))
     north_w[...] = jnp.sqrt(all_scaled * pltpu.roll(all_scaled, tall - 1, 0))
+    west_w[...] = lane_roll(east_w[...], 1)
+    south_w[...] = pltpu.roll(north_w[...], 1, 0)
+    diagonal[...] = surface_shift + ((east_w[...] + west_w[...]) + (north_w[...] + south_w[...]))
 
     for q in range(CHUNKS):
         for p in b_order:
@@ -414,24 +414,25 @@
     core = slice(BY - 8, 2 * BY + 8)
     height[...] = jnp.zeros(height.shape, jnp.float32)
 
-    for phase in range(4):
+    def group(step, count, phase):
         band = slice(8 * phase, tall - 8 * phase)
-        wide = tall - 16 * phase
-
-        def advance(step, carry, band=band, wide=wide, phase=phase):
-            now = direction[band, :]
-            inner = slice(BY - 8 - 8 * phase, BY - 8 - 8 * phase + BY + 16)
-            height[...] = height[...] + now[inner, :]
-            east_flux = east_w[band, :] * (now - lane_roll(now, -1))
-            north_flux = north_w[band, :] * (now - pltpu.roll(now, wide - 1, 0))
-            image = surface_shift * now + east_flux - lane_roll(east_flux, 1)
-            image = image + north_flux - pltpu.roll(north_flux, 1, 0)
-            left = residual[band, :] - image
-            residual[band, :] = left
-            direction[band, :] = table_ref[2 * step] * now + table_ref[2 * step + 1] * left
-            return carry
-
-        lax.fori_loop(8 * phase, min(8 * phase + 8, STEPS - 1), advance, 0)
+        rows = tall - 16 * phase
+        inner = slice(BY - 8 - 8 * phase, BY - 8 - 8 * phase + BY + 16)
+        now, left, total = direction[band, :], residual[band, :], height[...]
+        for i in range(count):
+            total = total + now[inner, :]
+            image = diagonal[band, :] * now
+            image = image - (east_w[band, :] * lane_roll(now, -1) + west_w[band, :] * lane_roll(now, 1))
+            image = image - (north_w[band, :] * pltpu.roll(now, rows - 1, 0) + south_w[band, :] * pltpu.roll(now, 1, 0))
+            left = left - image
+            now = table_ref[2 * (step + i)] * now + table_ref[2 * (step + i) + 1] * left
+        direction[band, :], residual[band, :], height[...] = now, left, total
+
+    for phase in range(3):
+        for half in range(2):
+            group(8 * phase + 4 * half, 4, phase)
+    group(24, 4, 3)
+    group(28, 3, 3)
     height[...] = height[...] + direction[core, :]
 
     def own_blocks(values):
@@ -485,6 +486,7 @@
     surface_ref[:, :BX], surface_ref[:, BX:] = own_heights
 
     ra_copies = [{} for _ in range(CHUNKS + 1)]
+    units(6, 8)
     for p in b_order:
         rb_copies[CHUNKS][p].wait()
     for p in range(B_SIZE):
@@ -582,6 +584,9 @@
             pltpu.VMEM(wide, f32),
             pltpu.VMEM(wide, f32),
             pltpu.VMEM((BY + 16, 3 * BX), f32),
+            pltpu.VMEM(wide, f32),
+            pltpu.VMEM(wide, f32),
+            pltpu.VMEM(wide, f32),
             [pltpu.VMEM((1 + 2 * B_SIZE, CH, BX), f32) for _ in range(CHUNKS)],
             pltpu.VMEM((B_SIZE, 8, BX), f32),
             pltpu.VMEM((1 + 2 * B_SIZE, 8, BX), f32),

time: 63 us -> 54.5 us (0.87)
  Pallas kernels: 62.2 us -> 53.7 us
    pallas_call x1, Pallas kernels: 58.1 us -> 49.6 us  [main_call(): pl.pallas_call(main_kernel, out_shape=(pltpu.VMEM((SLOTS, 2, LEV, BY, BX)...]
where the time goes in v3:
time: 54.5 us; the launch traced here: 54.4 us
  Pallas kernels  53.7 us (99%)
  between operations  0.66 us (1%)
    pallas_call x1, Pallas kernels, main_call(): pl.pallas_call(main_kernel, out_shape=(pltpu.VMEM((SLOTS, 2, LEV, BY, BX)...  49.6 us
    pallas_call x1, Pallas kernels, final_call(): pl.pallas_call(final_kernel, out_shape=(jax.ShapeDtypeStruct(deep, f32),...  4.09 us

profile of v3, /device:TPU:1, one launch (start us, length us, event | category | flops | bytes accessed | tf_op | source)
XLA Modules:
  0.0 54.4 jit_solution(17994713980292043837)
XLA Ops:
  0.6 0.0 copy-start
  0.6 49.6 %columns_and_surface.1 = (f32[4,2,62,32,128]{4,3,2,1,0:T(8,128)S(1)}, f32[4,2,32,128]{3,2,1,0:T(8,128)S(1)}, f32[4,2,32,128]{3,2,1,0:T(8,128)S(1)}, f32[4,32,128...) custom-call(s32[4]{0:T(128)} %ids_ref.1, f32[64]{0:T(128)} %constant.2.clone.table_ref, ...), custom_call_target="tpu_custom_call" | custom-call | tf_op jit(solution)/shard_map/columns_and_surface/pallas_call | solution.py:550
  50.3 0.0 copy-done
  50.3 4.1 %pressure_correction.1 = (f32[4,2,62,32,128]{4,3,2,1,0:T(8,128)}, f32[4,32,128]{2,1,0:T(8,128)}, f32[32,256]{1,0:T(8,128)}, f32[32,256]{1,0:T(8,128)}) custom-call(s32[4,32,128]{2,1,0:T(8,128)S(1)} %copy-done, f32[4,2,62,32,128]{4,3,2,1,0:T(8,128)S(1)} %get-tuple-element.10.mixed_ref, f32[4,2,32,128]{3,2,1,0:T(8,128)S(1)} %get-tuple-element.11.press_ref, ...), custom_call_target="tpu_custom_call" | custom-call | tf_op jit(solution)/shard_map/pressure_correction/pallas_call | solution.py:651
Async XLA Ops:
  0.6 49.6 %copy-start = (s32[4,32,128]{2,1,0:T(8,128)S(1)}, s32[4,32,128]{2,1,0:T(8,128)}, u32[]{:S(2)}) copy-start(s32[4,32,128]{2,1,0:T(8,128)} %count_ref.3) | copy-start | bytes 196612

commit v4 on v3

--- a/solution.py
+++ b/solution.py
@@ -17,8 +17,10 @@
 A_SIZE = NX_CHIPS * CORES
 B_SIZE = NY_CHIPS * NZ_CHIPS
 AROUND = ((-1, -1), (-1, 0), (-1, 1), (0, -1), (0, 1), (1, -1), (1, 0), (1, 1))
+SIDES = tuple(d for d in AROUND if d[0] != 0)
 UNIT = 16
 UNITS = SLOTS * BY // UNIT
+PIECES = 2
 
 mix_rate = 0.25
 drag_step = 0.5
@@ -121,7 +123,10 @@
     spread,
     gathered,
     source_own,
+    scaled_out,
     scaled_own,
+    result_out,
+    result_in,
     packed_scaled,
     packed_source,
     vert_scaled,
@@ -160,6 +165,8 @@
     rb_recv,
     ra_send,
     ra_recv,
+    place_send,
+    place_recv,
     local_sem,
 ):
     gx = lax.axis_index("gx")
@@ -185,14 +192,30 @@
         z = lax.rem(my_z + step_z, NZ_CHIPS)
         return (my_x * 2 + lax.div(z, 2), y * 4 + lax.rem(z, 2) * 2 + my_c)
 
+    def snake(y_grid, z):
+        return z + lax.rem(y_grid, 2) * (NZ_CHIPS - 1 - 2 * z)
+
+    def solver_of(lon, lat):
+        y_grid = lax.div(lat, NZ_CHIPS)
+        z = snake(y_grid, lax.rem(lat, NZ_CHIPS))
+        y = lax.rem(y_grid + NY_CHIPS - 1, NY_CHIPS)
+        return (lax.div(lon, 2) * 2 + lax.div(z, 2), y * 4 + lax.rem(z, 2) * 2 + lax.rem(lon, 2))
+
+    lon = my_x * 2 + my_c
+    my_y_grid = lax.rem(my_y + 1, NY_CHIPS)
+    lat = my_y_grid * NZ_CHIPS + snake(my_y_grid, my_z)
+
     def near(n):
         dx, dy = AROUND[n]
-        return (lax.rem(gx + dx + 8, 8), lax.rem(gy + dy + 16, 16))
+        return solver_of(lax.rem(lon + dx + 8, 8), lax.rem(lat + dy + 16, 16))
 
     def copy(src, dst, send, recv, to):
         return pltpu.make_async_remote_copy(
             src_ref=src, dst_ref=dst, send_sem=send, recv_sem=recv, device_id=to, device_id_type=MESH
         )
+
+    def arrived(whole, send, recv):
+        copy(whole, whole, send, recv, (gx, gy)).wait()
 
     a_order = sorted(range(1, A_SIZE), key=lambda o: -min(o // 2, NX_CHIPS - o // 2))
     b_order = sorted(
@@ -205,8 +228,8 @@
         part = (slice(None), slice(None), slice(None), pl.ds(q * CH, CH))
         loads.append(pltpu.make_async_copy(adjoint_hbm.at[part], mixed_ref.at[part], load_sem.at[q]))
     loads.append(pltpu.make_async_copy(velocity_hbm, velocity_ref, load_sem.at[CHUNKS]))
-    for c in loads:
-        c.start()
+    loads[0].start()
+    loads[1].start()
 
     barrier = pltpu.get_barrier_semaphore()
     for o in range(1, A_SIZE):
@@ -215,6 +238,8 @@
         pl.semaphore_signal(barrier, inc=1, device_id=b_peer(p, 1), device_id_type=MESH)
     for n in range(8):
         pl.semaphore_signal(barrier, inc=1, device_id=near(n), device_id_type=MESH)
+    pl.semaphore_signal(barrier, inc=1, device_id=solver_of(gx, gy), device_id_type=MESH)
+    pl.semaphore_signal(barrier, inc=1, device_id=(lon, lat), device_id_type=MESH)
 
     lane8 = lax.broadcasted_iota(jnp.int32, (8, BX), 1)
     lane32 = lax.broadcasted_iota(jnp.int32, (BY, BX), 1)
@@ -241,12 +266,9 @@
     def unpack(packed, base):
         return jnp.concatenate([lane_roll(packed, base - 32 * q) for q in range(4)], axis=0)
 
-    wet = mask_ref[...].astype(jnp.float32)
-    scaled = bathymetry_ref[...] * wet
-    scaled_own[0] = scaled[:, :BX]
-    scaled_own[1] = scaled[:, BX:]
-    packed_scaled[0] = pack(scaled_own[0], 0)
-    packed_scaled[1] = pack(scaled_own[1], 96)
+    scaled = bathymetry_ref[...] * mask_ref[...].astype(jnp.float32)
+    scaled_out[0] = scaled[:, :BX]
+    scaled_out[1] = scaled[:, BX:]
 
     def force(q):
         rows = slice(q * CH, (q + 1) * CH)
@@ -263,38 +285,38 @@
         lax.fori_loop(0, SLOTS, one, 0)
 
     loads[0].wait()
+    loads[2].start()
     force(0)
-    pl.semaphore_wait(barrier, A_SIZE - 1 + B_SIZE - 1 + 8)
-
-    id_copies = {}
+    pl.semaphore_wait(barrier, A_SIZE - 1 + B_SIZE - 1 + 8 + 2)
+
     for o in a_order:
-        id_copies[o] = copy(idbuf.at[0], idbuf.at[o], id_send.at[o], id_recv.at[o], a_peer(o, 1))
-        id_copies[o].start()
-
-    a_copies = [{} for _ in range(CHUNKS)]
-
+        copy(idbuf.at[0], idbuf.at[o], id_send.at[0], id_recv.at[0], a_peer(o, 1)).start()
+
+    place_copy = copy(scaled_out, scaled_own, place_send.at[0], place_recv.at[0], solver_of(gx, gy))
+    place_copy.start()
     def send_a(q):
         for o in a_order:
-            a_copies[q][o] = copy(
+            copy(
                 cand[q].at[pl.ds(1, SLOTS)],
                 cand[q].at[pl.ds(1 + SLOTS * o, SLOTS)],
-                a_send.at[q, o],
-                a_recv.at[q, o],
+                a_send.at[q],
+                a_recv.at[q],
                 a_peer(o, 1),
-            )
-            a_copies[q][o].start()
+            ).start()
 
     send_a(0)
 
-    def halo_copies(own, packed, vert, side, send, recv):
-        copies = []
+    def send_halo(own, packed, vert, side, send, recv):
         for n, (dx, dy) in enumerate(AROUND):
             if dx == 0:
-                src, dst = own, vert.at[0 if dy < 0 else 1]
-            else:
-                src, dst = packed.at[0 if dx < 0 else 1], side.at[n]
-            copies.append(copy(src, dst, send.at[n], recv.at[n], near(n)))
-        return copies
+                copy(own, vert.at[0 if dy < 0 else 1], send.at[0], recv.at[0], near(n)).start()
+        for n, (dx, dy) in enumerate(AROUND):
+            if dx != 0:
+                copy(packed.at[0 if dx < 0 else 1], side.at[SIDES.index((dx, dy))], send.at[1], recv.at[1], near(n)).start()
+
+    def halo_arrived(vert, side, send, recv):
+        arrived(vert, send.at[0], recv.at[0])
+        arrived(side, send.at[1], recv.at[1])
 
     def extended(own, vert, side):
         bands = []
@@ -305,9 +327,9 @@
             else:
                 k = 0 if dy > 0 else 1
                 left, right = vert[k, 0], vert[k, 1]
-                inside = jnp.where(gy + dy >= 0, 1.0, 0.0) * jnp.where(gy + dy < 16, 1.0, 0.0)
-            west = unpack(side[AROUND.index((1, -dy))], 32) * jnp.where(gx > 0, 1.0, 0.0)
-            east = unpack(side[AROUND.index((-1, -dy))], 64) * jnp.where(gx < 7, 1.0, 0.0)
+                inside = jnp.where(lat + dy >= 0, 1.0, 0.0) * jnp.where(lat + dy < 16, 1.0, 0.0)
+            west = unpack(side[SIDES.index((1, -dy))], 32) * jnp.where(lon > 0, 1.0, 0.0)
+            east = unpack(side[SIDES.index((-1, -dy))], 64) * jnp.where(lon < 7, 1.0, 0.0)
             left, right = lane_roll(left, 64), lane_roll(right, 64)
             first = jnp.where(lane32 < 32, 0.0, jnp.where(lane32 < 64, west, left))
             middle = jnp.where(lane32 < 64, left, right)
@@ -324,23 +346,25 @@
 
     for q in range(1, CHUNKS):
         loads[q].wait()
+        if q + 2 <= CHUNKS:
+            loads[q + 2].start()
         force(q)
         send_a(q)
 
-    scaled_copies = halo_copies(scaled_own, packed_scaled, vert_scaled, side_scaled, h_send, h_recv)
-    for c in scaled_copies:
-        c.start()
+    place_copy.wait()
+    packed_scaled[0] = pack(scaled_own[0], 0)
+    packed_scaled[1] = pack(scaled_own[1], 96)
+    send_halo(scaled_own, packed_scaled, vert_scaled, side_scaled, h_send, h_recv)
 
     loads[CHUNKS].wait()
     units(0, 2)
-    for o in a_order:
-        id_copies[o].wait()
+    arrived(idbuf.at[pl.ds(1, A_SIZE - 1)], id_send.at[0], id_recv.at[0])
     spot = lax.broadcasted_iota(jnp.int32, (2 * B_SIZE, BX), 0)
     spot_lane = lax.broadcasted_iota(jnp.int32, (2 * B_SIZE, BX), 1)
     spot_p = spot // 2
-    spot_y = (my_y + spot_p // NZ_CHIPS) % NY_CHIPS
+    spot_y = (my_y + spot_p // NZ_CHIPS + 1) % NY_CHIPS
     spot_z = (my_z + spot_p % NZ_CHIPS) % NZ_CHIPS
-    owner = (my_x * 2 + spot_z // 2) * 16 + spot_y * 4 + (spot_z % 2) * 2 + my_c
+    owner = lon * 16 + spot_y * NZ_CHIPS + spot_z + (spot_y % 2) * (NZ_CHIPS - 1 - 2 * spot_z)
     target = owner * 2 + spot % 2
     forward = jnp.zeros((2 * B_SIZE, BX), jnp.int32)
     for o in range(A_SIZE):
@@ -365,22 +389,16 @@
     def back_of(o, s):
         return jnp.clip(back_idx[o, s], 0, 2 * B_SIZE)
 
-    b_copies = [{} for _ in range(CHUNKS)]
     for q in range(CHUNKS):
-        for o in a_order:
-            a_copies[q][o].wait()
+        arrived(cand[q].at[pl.ds(1 + SLOTS, SLOTS * (A_SIZE - 1))], a_send.at[q], a_recv.at[q])
         for p in b_order + [0]:
             for h in range(2):
                 spread[q, p, h] = cand[q][picked(2 * p + h)]
             if p > 0:
-                b_copies[q][p] = copy(
-                    spread.at[q, p], gathered.at[q, p], b_send.at[q, p], b_recv.at[q, p], b_peer(p, 1)
-                )
-                b_copies[q][p].start()
+                copy(spread.at[q, p], gathered.at[q, p], b_send.at[q], b_recv.at[q], b_peer(p, 1)).start()
 
     units(2, 6)
-    for c in scaled_copies:
-        c.wait()
+    halo_arrived(vert_scaled, side_scaled, h_send, h_recv)
     scaled_ext[...] = extended(scaled_own, vert_scaled, side_scaled)
     all_scaled = scaled_ext[...]
     tall = all_scaled.shape[0]
@@ -391,22 +409,18 @@
     diagonal[...] = surface_shift + ((east_w[...] + west_w[...]) + (north_w[...] + south_w[...]))
 
     for q in range(CHUNKS):
-        for p in b_order:
-            b_copies[q][p].wait()
+        arrived(gathered.at[q, pl.ds(1, B_SIZE - 1)], b_send.at[q], b_recv.at[q])
         rows = slice(q * CH, (q + 1) * CH)
         for h in range(2):
             total = spread[q, 0, h]
             for p in range(1, B_SIZE):
                 total = total + gathered[q, p, h]
-            source_own[h, rows, :] = total * wet[rows, h * BX : (h + 1) * BX]
+            source_own[h, rows, :] = jnp.where(scaled_own[h, rows, :] > 0.0, total, 0.0)
 
     packed_source[0] = pack(source_own[0], 0)
     packed_source[1] = pack(source_own[1], 96)
-    source_copies = halo_copies(source_own, packed_source, vert_source, side_source, g_send, g_recv)
-    for c in source_copies:
-        c.start()
-    for c in source_copies:
-        c.wait()
+    send_halo(source_own, packed_source, vert_source, side_source, g_send, g_recv)
+    halo_arrived(vert_source, side_source, g_send, g_recv)
     start = extended(source_own, vert_source, side_source)
     centre, _ = chebyshev_table(STEPS)
     residual[...] = start
@@ -429,10 +443,8 @@
         direction[band, :], residual[band, :], height[...] = now, left, total
 
     for phase in range(3):
-        for half in range(2):
-            group(8 * phase + 4 * half, 4, phase)
-    group(24, 4, 3)
-    group(28, 3, 3)
+        group(8 * phase, 8, phase)
+    group(24, 7, 3)
     height[...] = height[...] + direction[core, :]
 
     def own_blocks(values):
@@ -454,22 +466,17 @@
             returned[q][1 + h] = own_heights[h][q * CH : (q + 1) * CH, :]
     edge_pairs[0] = pair
 
-    rb_copies = [{} for _ in range(CHUNKS + 1)]
     for p in b_order:
-        rb_copies[CHUNKS][p] = copy(
-            edge_pairs.at[0], edge_pairs.at[p], rb_send.at[CHUNKS, p], rb_recv.at[CHUNKS, p], b_peer(p, -1)
-        )
-        rb_copies[CHUNKS][p].start()
+        copy(edge_pairs.at[0], edge_pairs.at[p], rb_send.at[CHUNKS], rb_recv.at[CHUNKS], b_peer(p, -1)).start()
     for q in range(CHUNKS):
         for p in b_order:
-            rb_copies[q][p] = copy(
+            copy(
                 returned[q].at[pl.ds(1, 2)],
                 returned[q].at[pl.ds(1 + 2 * p, 2)],
-                rb_send.at[q, p],
-                rb_recv.at[q, p],
+                rb_send.at[q],
+                rb_recv.at[q],
                 b_peer(p, -1),
-            )
-            rb_copies[q][p].start()
+            ).start()
 
     east_step = lane_roll(mid, -1) - mid
     north_step = height[9 : BY + 9, :] - mid
@@ -482,13 +489,12 @@
         + north_w[BY - 1 : 2 * BY - 1, :] * south_step * south_step
     )
     sens = 0.25 * total / jnp.maximum(scaled_ext[BY : 2 * BY, :], 0.25)
-    sens_ref[:, :BX], sens_ref[:, BX:] = own_blocks(sens)
-    surface_ref[:, :BX], surface_ref[:, BX:] = own_heights
-
-    ra_copies = [{} for _ in range(CHUNKS + 1)]
+    for h, (sens_part, height_part) in enumerate(zip(own_blocks(sens), own_heights)):
+        result_out[0, :, h * BX : (h + 1) * BX] = height_part
+        result_out[1, :, h * BX : (h + 1) * BX] = sens_part
+
     units(6, 8)
-    for p in b_order:
-        rb_copies[CHUNKS][p].wait()
+    arrived(edge_pairs.at[pl.ds(1, B_SIZE - 1)], rb_send.at[CHUNKS], rb_recv.at[CHUNKS])
     for p in range(B_SIZE):
         both = edge_pairs[p]
         edges[1 + 2 * p] = jnp.where(row8 < 2, both, 0.0)
@@ -499,36 +505,32 @@
             tile = tile + pltpu.roll(edges[back_of(o, s)], 2 * s, 0)
         edge_out[o] = tile
         if o > 0:
-            ra_copies[CHUNKS][o] = copy(
-                edge_out.at[o], edge_in.at[o], ra_send.at[CHUNKS, o], ra_recv.at[CHUNKS, o], a_peer(o, -1)
-            )
-            ra_copies[CHUNKS][o].start()
+            copy(edge_out.at[o], edge_in.at[o], ra_send.at[CHUNKS], ra_recv.at[CHUNKS], a_peer(o, -1)).start()
     for q in range(CHUNKS):
-        for p in b_order:
-            rb_copies[q][p].wait()
+        arrived(returned[q].at[pl.ds(3, 2 * (B_SIZE - 1))], rb_send.at[q], rb_recv.at[q])
         for o in a_order + [0]:
             for s in range(SLOTS):
                 slot_out[q, o, s] = returned[q][back_of(o, s)]
             if o > 0:
-                ra_copies[q][o] = copy(
-                    slot_out.at[q, o], slot_in.at[q, o], ra_send.at[q, o], ra_recv.at[q, o], a_peer(o, -1)
-                )
-                ra_copies[q][o].start()
-    for o in a_order:
-        ra_copies[CHUNKS][o].wait()
+                copy(slot_out.at[q, o], slot_in.at[q, o], ra_send.at[q], ra_recv.at[q], a_peer(o, -1)).start()
+    result_copy = copy(result_out, result_in, place_send.at[1], place_recv.at[1], (lon, lat))
+    result_copy.start()
+    arrived(edge_in.at[pl.ds(1, A_SIZE - 1)], ra_send.at[CHUNKS], ra_recv.at[CHUNKS])
     edge = edge_out[0]
     for o in range(1, A_SIZE):
         edge = edge + edge_in[o]
     for s in range(SLOTS):
         slot_sum[s, BY : BY + 8, :] = edge if s == 0 else pltpu.roll(edge, 8 - 2 * s, 0)
     for q in range(CHUNKS):
-        for o in a_order:
-            ra_copies[q][o].wait()
+        arrived(slot_in.at[q, pl.ds(1, A_SIZE - 1)], ra_send.at[q], ra_recv.at[q])
         for s in range(SLOTS):
             total = slot_out[q, 0, s]
             for o in range(1, A_SIZE):
                 total = total + slot_in[q, o, s]
             slot_sum[s, q * CH : (q + 1) * CH, :] = total
+    result_copy.wait()
+    surface_ref[...] = result_in[0]
+    sens_ref[...] = result_in[1]
     for s in range(SLOTS):
         here = slot_sum[s, 0:BY, :]
         flat = jnp.broadcast_to(slot_sum[s, BY + 1 : BY + 2, :], (BY, BX))
@@ -572,12 +574,15 @@
             pltpu.VMEM((CHUNKS, B_SIZE, 2, CH, BX), f32),
             pltpu.VMEM((2, BY, BX), f32),
             pltpu.VMEM((2, BY, BX), f32),
+            pltpu.VMEM((2, BY, BX), f32),
+            pltpu.VMEM((2, BY, 2 * BX), f32),
+            pltpu.VMEM((2, BY, 2 * BX), f32),
             pltpu.VMEM((2, 8, BX), f32),
             pltpu.VMEM((2, 8, BX), f32),
             pltpu.VMEM((2, 2, BY, BX), f32),
             pltpu.VMEM((2, 2, BY, BX), f32),
-            pltpu.VMEM((8, 8, BX), f32),
-            pltpu.VMEM((8, 8, BX), f32),
+            pltpu.VMEM((len(SIDES), 8, BX), f32),
+            pltpu.VMEM((len(SIDES), 8, BX), f32),
             pltpu.VMEM(wide, f32),
             pltpu.VMEM(wide, f32),
             pltpu.VMEM(wide, f32),
@@ -596,20 +601,22 @@
             pltpu.VMEM((A_SIZE, 8, BX), f32),
             pltpu.VMEM((SLOTS, BY + 8, BX), f32),
             dma((CHUNKS + 1,)),
-            dma((A_SIZE,)),
-            dma((A_SIZE,)),
-            dma((CHUNKS, A_SIZE)),
-            dma((CHUNKS, A_SIZE)),
-            dma((CHUNKS, B_SIZE)),
-            dma((CHUNKS, B_SIZE)),
-            dma((8,)),
-            dma((8,)),
-            dma((8,)),
-            dma((8,)),
-            dma((CHUNKS + 1, B_SIZE)),
-            dma((CHUNKS + 1, B_SIZE)),
-            dma((CHUNKS + 1, A_SIZE)),
-            dma((CHUNKS + 1, A_SIZE)),
+            dma((1,)),
+            dma((1,)),
+            dma((CHUNKS,)),
+            dma((CHUNKS,)),
+            dma((CHUNKS,)),
+            dma((CHUNKS,)),
+            dma((2,)),
+            dma((2,)),
+            dma((2,)),
+            dma((2,)),
+            dma((CHUNKS + 1,)),
+            dma((CHUNKS + 1,)),
+            dma((CHUNKS + 1,)),
+            dma((CHUNKS + 1,)),
+            dma((2,)),
+            dma((2,)),
             dma((2,)),
         ],
         compiler_params=pltpu.CompilerParams(
@@ -621,25 +628,24 @@
 
 def final_kernel(
     count_ref, mixed_ref, press_ref, pull_ref, drag_ref, surface_ref, sens_ref,
-    out_hbm, drag_out_ref, surface_out_ref, sens_out_ref, stage, sems,
+    out_hbm, drag_out_ref, surface_out_ref, sens_out_ref, stage, sems, small_sems,
 ):
-    drag_out_ref[...] = drag_ref[...]
-    surface_out_ref[...] = surface_ref[...]
-    sens_out_ref[...] = sens_ref[...]
-    puts = []
-    for unit in range(UNITS):
-        slot, rows = unit // (BY // UNIT), slice(unit % (BY // UNIT) * UNIT, unit % (BY // UNIT) * UNIT + UNIT)
-        levels = count_ref[slot, rows, :]
-        press = [press_ref[slot, c, rows, :] for c in range(2)]
-        bed = [press[c] + pull_ref[slot, c, rows, :] for c in range(2)]
-        for k in range(LEV):
-            wet, bottom = levels > k, levels == k + 1
-            for c in range(2):
-                less = jnp.where(bottom, bed[c], jnp.where(wet, press[c], 0.0))
-                stage[slot, c, k, rows, :] = mixed_ref[slot, c, k, rows, :] - less
-        part = (slot, slice(None), slice(None), pl.ds(unit % (BY // UNIT) * UNIT, UNIT))
-        puts.append(pltpu.make_async_copy(stage.at[part], out_hbm.at[part], sems.at[unit]))
-        puts[-1].start()
+    small = ((drag_ref, drag_out_ref), (surface_ref, surface_out_ref), (sens_ref, sens_out_ref))
+    puts = [pltpu.make_async_copy(src, dst, small_sems.at[i]) for i, (src, dst) in enumerate(small)]
+    for c in puts:
+        c.start()
+    for slot in range(SLOTS):
+        levels = count_ref[slot]
+        for c in range(2):
+            press = press_ref[slot, c]
+            bed = press + pull_ref[slot, c]
+            for piece in range(PIECES):
+                for k in range(piece * LEV // PIECES, (piece + 1) * LEV // PIECES):
+                    less = jnp.where(levels == k + 1, bed, jnp.where(levels > k, press, 0.0))
+                    stage[slot, c, k] = mixed_ref[slot, c, k] - less
+                part = (slot, c, pl.ds(piece * LEV // PIECES, LEV // PIECES))
+                puts.append(pltpu.make_async_copy(stage.at[part], out_hbm.at[part], sems.at[len(puts) - len(small)]))
+                puts[-1].start()
     for c in puts:
         c.wait()
 
@@ -657,8 +663,8 @@
             jax.ShapeDtypeStruct(sens.shape, f32),
         ),
         in_specs=[vmem] * 7,
-        out_specs=(pl.BlockSpec(memory_space=pltpu.HBM), vmem, vmem, vmem),
-        scratch_shapes=[pltpu.VMEM(deep, f32), pltpu.SemaphoreType.DMA((UNITS,))],
+        out_specs=(pl.BlockSpec(memory_space=pltpu.HBM),) * 4,
+        scratch_shapes=[pltpu.VMEM(deep, f32), pltpu.SemaphoreType.DMA((SLOTS * 2 * PIECES,)), pltpu.SemaphoreType.DMA((3,))],
         compiler_params=pltpu.CompilerParams(vmem_limit_bytes=24 * 2**20),
         name="pressure_correction",
     )(level_count, mixed, press, pull, drag_grad, surface, sens)

time: 54.5 us -> 50 us (0.917)
  Pallas kernels: 53.7 us -> 49.2 us
    pallas_call x1, Pallas kernels: 49.6 us -> 45.7 us  [main_call(): pl.pallas_call(main_kernel, out_shape=(pltpu.VMEM((SLOTS, 2, LEV, BY, BX)...]
    pallas_call x1, Pallas kernels: 4.09 us -> 3.51 us  [final_call(): pl.pallas_call(final_kernel, out_shape=(jax.ShapeDtypeStruct(deep, f32),...]
where the time goes in v4:
time: 50 us; the launch traced here: 49.9 us
  Pallas kernels  49.2 us (98%)
  between operations  0.66 us (1%)
    pallas_call x1, Pallas kernels, main_call(): pl.pallas_call(main_kernel, out_shape=(pltpu.VMEM((SLOTS, 2, LEV, BY, BX)...  45.7 us
    pallas_call x1, Pallas kernels, final_call(): pl.pallas_call(final_kernel, out_shape=(jax.ShapeDtypeStruct(deep, f32),...  3.51 us

profile of v4, /device:TPU:1, one launch (start us, length us, event | category | flops | bytes accessed | tf_op | source)
XLA Modules:
  0.0 49.9 jit_solution(3889964441612896640)
XLA Ops:
  0.6 0.0 copy-start
  0.6 45.7 %columns_and_surface.1 = (f32[4,2,62,32,128]{4,3,2,1,0:T(8,128)S(1)}, f32[4,2,32,128]{3,2,1,0:T(8,128)S(1)}, f32[4,2,32,128]{3,2,1,0:T(8,128)S(1)}, f32[4,32,128...) custom-call(s32[4]{0:T(128)} %ids_ref.1, f32[64]{0:T(128)} %constant.2.clone.table_ref, ...), custom_call_target="tpu_custom_call" | custom-call | tf_op jit(solution)/shard_map/columns_and_surface/pallas_call | solution.py:552
  46.3 0.0 copy-done
  46.4 3.5 %pressure_correction.1 = (f32[4,2,62,32,128]{4,3,2,1,0:T(8,128)}, f32[4,32,128]{2,1,0:T(8,128)}, f32[32,256]{1,0:T(8,128)}, f32[32,256]{1,0:T(8,128)}) custom-call(s32[4,32,128]{2,1,0:T(8,128)S(1)} %copy-done, f32[4,2,62,32,128]{4,3,2,1,0:T(8,128)S(1)} %get-tuple-element.10.mixed_ref, f32[4,2,32,128]{3,2,1,0:T(8,128)S(1)} %get-tuple-element.11.press_ref, ...), custom_call_target="tpu_custom_call" | custom-call | tf_op jit(solution)/shard_map/pressure_correction/pallas_call | solution.py:657
Async XLA Ops:
  0.6 45.7 %copy-start = (s32[4,32,128]{2,1,0:T(8,128)S(1)}, s32[4,32,128]{2,1,0:T(8,128)}, u32[]{:S(2)}) copy-start(s32[4,32,128]{2,1,0:T(8,128)} %count_ref.3) | copy-start | bytes 196612

commit v5 on v4

--- a/solution.py
+++ b/solution.py
@@ -98,12 +98,11 @@
 
 
 def main_kernel(
-    ids_ref,
-    table_ref,
-    count_ref,
-    drag_ref,
-    bathymetry_ref,
-    mask_ref,
+    ids_hbm,
+    count_hbm,
+    drag_hbm,
+    bathymetry_hbm,
+    mask_hbm,
     adjoint_hbm,
     velocity_hbm,
     mixed_ref,
@@ -114,6 +113,11 @@
     sens_ref,
     levels_ref,
     velocity_ref,
+    ids_ref,
+    count_ref,
+    drag_ref,
+    bathymetry_ref,
+    mask_ref,
     idbuf,
     forward_vec,
     back_vec,
@@ -139,8 +143,6 @@
     direction,
     residual,
     height,
-    west_w,
-    south_w,
     diagonal,
     returned,
     edge_pairs,
@@ -168,6 +170,7 @@
     place_send,
     place_recv,
     local_sem,
+    small_sem,
 ):
     gx = lax.axis_index("gx")
     gy = lax.axis_index("gy")
@@ -228,14 +231,26 @@
         part = (slice(None), slice(None), slice(None), pl.ds(q * CH, CH))
         loads.append(pltpu.make_async_copy(adjoint_hbm.at[part], mixed_ref.at[part], load_sem.at[q]))
     loads.append(pltpu.make_async_copy(velocity_hbm, velocity_ref, load_sem.at[CHUNKS]))
+    pairs = (
+        (ids_hbm, ids_ref),
+        (count_hbm, count_ref),
+        (bathymetry_hbm, bathymetry_ref),
+        (mask_hbm, mask_ref),
+        (drag_hbm, drag_ref),
+    )
+    small = [pltpu.make_async_copy(src, dst, small_sem.at[i]) for i, (src, dst) in enumerate(pairs)]
+    small[0].start()
+    small[1].start()
     loads[0].start()
+    for c in small[2:]:
+        c.start()
     loads[1].start()
 
     barrier = pltpu.get_barrier_semaphore()
-    for o in range(1, A_SIZE):
+    for p in b_order:
+        pl.semaphore_signal(barrier, inc=1, device_id=b_peer(p, 1), device_id_type=MESH)
+    for o in a_order:
         pl.semaphore_signal(barrier, inc=1, device_id=a_peer(o, 1), device_id_type=MESH)
-    for p in range(1, B_SIZE):
-        pl.semaphore_signal(barrier, inc=1, device_id=b_peer(p, 1), device_id_type=MESH)
     for n in range(8):
         pl.semaphore_signal(barrier, inc=1, device_id=near(n), device_id_type=MESH)
     pl.semaphore_signal(barrier, inc=1, device_id=solver_of(gx, gy), device_id_type=MESH)
@@ -246,6 +261,8 @@
     row8 = lax.broadcasted_iota(jnp.int32, (8, BX), 0)
     row32 = lax.broadcasted_iota(jnp.int32, (BY, BX), 0)
 
+    small[0].wait()
+    small[1].wait()
     id_row = jnp.full((8, BX), -1, jnp.int32)
     for s in range(SLOTS):
         id_row = jnp.where(lane8 == s, ids_ref[s], id_row)
@@ -266,6 +283,8 @@
     def unpack(packed, base):
         return jnp.concatenate([lane_roll(packed, base - 32 * q) for q in range(4)], axis=0)
 
+    small[2].wait()
+    small[3].wait()
     scaled = bathymetry_ref[...] * mask_ref[...].astype(jnp.float32)
     scaled_out[0] = scaled[:, :BX]
     scaled_out[1] = scaled[:, BX:]
@@ -351,13 +370,6 @@
         force(q)
         send_a(q)
 
-    place_copy.wait()
-    packed_scaled[0] = pack(scaled_own[0], 0)
-    packed_scaled[1] = pack(scaled_own[1], 96)
-    send_halo(scaled_own, packed_scaled, vert_scaled, side_scaled, h_send, h_recv)
-
-    loads[CHUNKS].wait()
-    units(0, 2)
     arrived(idbuf.at[pl.ds(1, A_SIZE - 1)], id_send.at[0], id_recv.at[0])
     spot = lax.broadcasted_iota(jnp.int32, (2 * B_SIZE, BX), 0)
     spot_lane = lax.broadcasted_iota(jnp.int32, (2 * B_SIZE, BX), 1)
@@ -389,6 +401,11 @@
     def back_of(o, s):
         return jnp.clip(back_idx[o, s], 0, 2 * B_SIZE)
 
+    place_copy.wait()
+    packed_scaled[0] = pack(scaled_own[0], 0)
+    packed_scaled[1] = pack(scaled_own[1], 96)
+    send_halo(scaled_own, packed_scaled, vert_scaled, side_scaled, h_send, h_recv)
+
     for q in range(CHUNKS):
         arrived(cand[q].at[pl.ds(1 + SLOTS, SLOTS * (A_SIZE - 1))], a_send.at[q], a_recv.at[q])
         for p in b_order + [0]:
@@ -397,16 +414,17 @@
             if p > 0:
                 copy(spread.at[q, p], gathered.at[q, p], b_send.at[q], b_recv.at[q], b_peer(p, 1)).start()
 
-    units(2, 6)
+    small[4].wait()
+    loads[CHUNKS].wait()
+    units(0, 6)
     halo_arrived(vert_scaled, side_scaled, h_send, h_recv)
     scaled_ext[...] = extended(scaled_own, vert_scaled, side_scaled)
     all_scaled = scaled_ext[...]
     tall = all_scaled.shape[0]
     east_w[...] = jnp.sqrt(all_scaled * lane_roll(all_scaled, -1))
     north_w[...] = jnp.sqrt(all_scaled * pltpu.roll(all_scaled, tall - 1, 0))
-    west_w[...] = lane_roll(east_w[...], 1)
-    south_w[...] = pltpu.roll(north_w[...], 1, 0)
-    diagonal[...] = surface_shift + ((east_w[...] + west_w[...]) + (north_w[...] + south_w[...]))
+    east, north = east_w[...], north_w[...]
+    diagonal[...] = surface_shift + ((east + lane_roll(east, 1)) + (north + pltpu.roll(north, 1, 0)))
 
     for q in range(CHUNKS):
         arrived(gathered.at[q, pl.ds(1, B_SIZE - 1)], b_send.at[q], b_recv.at[q])
@@ -422,7 +440,7 @@
     send_halo(source_own, packed_source, vert_source, side_source, g_send, g_recv)
     halo_arrived(vert_source, side_source, g_send, g_recv)
     start = extended(source_own, vert_source, side_source)
-    centre, _ = chebyshev_table(STEPS)
+    centre, table = chebyshev_table(STEPS)
     residual[...] = start
     direction[...] = start / centre
     core = slice(BY - 8, 2 * BY + 8)
@@ -435,11 +453,13 @@
         now, left, total = direction[band, :], residual[band, :], height[...]
         for i in range(count):
             total = total + now[inner, :]
+            east, north = east_w[band, :], north_w[band, :]
             image = diagonal[band, :] * now
-            image = image - (east_w[band, :] * lane_roll(now, -1) + west_w[band, :] * lane_roll(now, 1))
-            image = image - (north_w[band, :] * pltpu.roll(now, rows - 1, 0) + south_w[band, :] * pltpu.roll(now, 1, 0))
+            image = image - (east * lane_roll(now, -1) + lane_roll(east * now, 1))
+            image = image - (north * pltpu.roll(now, rows - 1, 0) + pltpu.roll(north * now, 1, 0))
             left = left - image
-            now = table_ref[2 * (step + i)] * now + table_ref[2 * (step + i) + 1] * left
+            carry, push = table[step + i]
+            now = carry * now + push * left
         direction[band, :], residual[band, :], height[...] = now, left, total
 
     for phase in range(3):
@@ -541,13 +561,10 @@
 
 
 def main_call(block_ids, level_count, drag_coef, bathymetry, land_mask, adjoint_vel, velocity):
-    _, table = chebyshev_table(STEPS)
-    flat_table = jnp.array([v for pair in table for v in pair], jnp.float32)
     f32, i32 = jnp.float32, jnp.int32
     wide = (3 * BY, 3 * BX)
     dma = pltpu.SemaphoreType.DMA
     vmem = pl.BlockSpec(memory_space=pltpu.VMEM)
-    smem = pl.BlockSpec(memory_space=pltpu.SMEM)
     hbm = pl.BlockSpec(memory_space=pltpu.HBM)
     return pl.pallas_call(
         main_kernel,
@@ -559,11 +576,16 @@
             pltpu.VMEM((BY, 2 * BX), f32),
             pltpu.VMEM((BY, 2 * BX), f32),
         ),
-        in_specs=[smem, smem, vmem, vmem, vmem, vmem, hbm, hbm],
+        in_specs=[hbm] * 7,
         out_specs=(vmem,) * 6,
         scratch_shapes=[
             pltpu.VMEM((SLOTS, BY, BX), i32),
             pltpu.VMEM((SLOTS, 2, LEV, BY, BX), jnp.bfloat16),
+            pltpu.SMEM((SLOTS,), i32),
+            pltpu.VMEM((SLOTS, BY, BX), i32),
+            pltpu.VMEM((SLOTS, BY, BX), f32),
+            pltpu.VMEM((BY, 2 * BX), f32),
+            pltpu.VMEM((BY, 2 * BX), i32),
             pltpu.VMEM((A_SIZE, 8, BX), i32),
             pltpu.VMEM((2 * B_SIZE, BX), i32),
             pltpu.VMEM((A_SIZE, BX), i32),
@@ -589,8 +611,6 @@
             pltpu.VMEM(wide, f32),
             pltpu.VMEM(wide, f32),
             pltpu.VMEM((BY + 16, 3 * BX), f32),
-            pltpu.VMEM(wide, f32),
-            pltpu.VMEM(wide, f32),
             pltpu.VMEM(wide, f32),
             [pltpu.VMEM((1 + 2 * B_SIZE, CH, BX), f32) for _ in range(CHUNKS)],
             pltpu.VMEM((B_SIZE, 8, BX), f32),
@@ -618,12 +638,13 @@
             dma((2,)),
             dma((2,)),
             dma((2,)),
+            dma((5,)),
         ],
         compiler_params=pltpu.CompilerParams(
             collective_id=0, has_side_effects=True, vmem_limit_bytes=50 * 2**20
         ),
         name="columns_and_surface",
-    )(block_ids, flat_table, level_count, drag_coef, bathymetry, land_mask, adjoint_vel, velocity)
+    )(block_ids, level_count, drag_coef, bathymetry, land_mask, adjoint_vel, velocity)
 
 
 def final_kernel(

time: 50 us -> 49 us (0.980)
  Pallas kernels: 49.2 us -> 48.2 us
    pallas_call x1, Pallas kernels: 45.7 us -> 44.7 us  [main_call(): pl.pallas_call(main_kernel, out_shape=(pltpu.VMEM((SLOTS, 2, LEV, BY, BX)...]
where the time goes in v5:
time: 49 us; the launch traced here: 48.9 us
  Pallas kernels  48.2 us (98%)
  between operations  0.66 us (1%)
    pallas_call x1, Pallas kernels, main_call(): pl.pallas_call(main_kernel, out_shape=(pltpu.VMEM((SLOTS, 2, LEV, BY, BX)...  44.7 us
    pallas_call x1, Pallas kernels, final_call(): pl.pallas_call(final_kernel, out_shape=(jax.ShapeDtypeStruct(deep, f32),...  3.51 us

profile of v5, /device:TPU:1, one launch (start us, length us, event | category | flops | bytes accessed | tf_op | source)
XLA Modules:
  0.0 48.9 jit_solution(14355296136638983920)
XLA Ops:
  0.6 0.0 copy-start
  0.6 44.7 %columns_and_surface.1 = (f32[4,2,62,32,128]{4,3,2,1,0:T(8,128)S(1)}, f32[4,2,32,128]{3,2,1,0:T(8,128)S(1)}, f32[4,2,32,128]{3,2,1,0:T(8,128)S(1)}, f32[4,32,128...) custom-call(s32[4]{0:T(128)} %ids_hbm.1, s32[4,32,128]{2,1,0:T(8,128)} %count_ref.1, ...), custom_call_target="tpu_custom_call" | custom-call | tf_op jit(solution)/shard_map/columns_and_surface/pallas_call | solution.py:569
  45.4 0.0 copy-done
  45.4 3.5 %pressure_correction.1 = (f32[4,2,62,32,128]{4,3,2,1,0:T(8,128)}, f32[4,32,128]{2,1,0:T(8,128)}, f32[32,256]{1,0:T(8,128)}, f32[32,256]{1,0:T(8,128)}) custom-call(s32[4,32,128]{2,1,0:T(8,128)S(1)} %copy-done, f32[4,2,62,32,128]{4,3,2,1,0:T(8,128)S(1)} %get-tuple-element.10.mixed_ref, f32[4,2,32,128]{3,2,1,0:T(8,128)S(1)} %get-tuple-element.11.press_ref, ...), custom_call_target="tpu_custom_call" | custom-call | tf_op jit(solution)/shard_map/pressure_correction/pallas_call | solution.py:678
Async XLA Ops:
  0.6 44.7 %copy-start = (s32[4,32,128]{2,1,0:T(8,128)S(1)}, s32[4,32,128]{2,1,0:T(8,128)}, u32[]{:S(2)}) copy-start(s32[4,32,128]{2,1,0:T(8,128)} %count_ref.1) | copy-start | bytes 196612

commit v6 on v5

--- a/solution.py
+++ b/solution.py
@@ -242,9 +242,6 @@
     small[0].start()
     small[1].start()
     loads[0].start()
-    for c in small[2:]:
-        c.start()
-    loads[1].start()
 
     barrier = pltpu.get_barrier_semaphore()
     for p in b_order:
@@ -255,6 +252,10 @@
         pl.semaphore_signal(barrier, inc=1, device_id=near(n), device_id_type=MESH)
     pl.semaphore_signal(barrier, inc=1, device_id=solver_of(gx, gy), device_id_type=MESH)
     pl.semaphore_signal(barrier, inc=1, device_id=(lon, lat), device_id_type=MESH)
+
+    for c in small[2:]:
+        c.start()
+    loads[1].start()
 
     lane8 = lax.broadcasted_iota(jnp.int32, (8, BX), 1)
     lane32 = lax.broadcasted_iota(jnp.int32, (BY, BX), 1)
@@ -327,11 +328,11 @@
 
     def send_halo(own, packed, vert, side, send, recv):
         for n, (dx, dy) in enumerate(AROUND):
+            if dx != 0:
+                copy(packed.at[0 if dx < 0 else 1], side.at[SIDES.index((dx, dy))], send.at[1], recv.at[1], near(n)).start()
+        for n, (dx, dy) in enumerate(AROUND):
             if dx == 0:
                 copy(own, vert.at[0 if dy < 0 else 1], send.at[0], recv.at[0], near(n)).start()
-        for n, (dx, dy) in enumerate(AROUND):
-            if dx != 0:
-                copy(packed.at[0 if dx < 0 else 1], side.at[SIDES.index((dx, dy))], send.at[1], recv.at[1], near(n)).start()
 
     def halo_arrived(vert, side, send, recv):
         arrived(vert, send.at[0], recv.at[0])
@@ -484,7 +485,7 @@
         pair = jnp.where(row8 == 2 * h, next_row, jnp.where(row8 == 2 * h + 1, flat, pair))
         for q in range(CHUNKS):
             returned[q][1 + h] = own_heights[h][q * CH : (q + 1) * CH, :]
-    edge_pairs[0] = pair
+    edge_pairs[0] = pair[0:4, :]
 
     for p in b_order:
         copy(edge_pairs.at[0], edge_pairs.at[p], rb_send.at[CHUNKS], rb_recv.at[CHUNKS], b_peer(p, -1)).start()
@@ -516,7 +517,7 @@
     units(6, 8)
     arrived(edge_pairs.at[pl.ds(1, B_SIZE - 1)], rb_send.at[CHUNKS], rb_recv.at[CHUNKS])
     for p in range(B_SIZE):
-        both = edge_pairs[p]
+        both = jnp.concatenate([edge_pairs[p], jnp.zeros((4, BX), jnp.float32)], axis=0)
         edges[1 + 2 * p] = jnp.where(row8 < 2, both, 0.0)
         edges[2 + 2 * p] = jnp.where(row8 < 2, pltpu.roll(both, 6, 0), 0.0)
     for o in a_order + [0]:
@@ -613,7 +614,7 @@
             pltpu.VMEM((BY + 16, 3 * BX), f32),
             pltpu.VMEM(wide, f32),
             [pltpu.VMEM((1 + 2 * B_SIZE, CH, BX), f32) for _ in range(CHUNKS)],
-            pltpu.VMEM((B_SIZE, 8, BX), f32),
+            pltpu.VMEM((B_SIZE, 4, BX), f32),
             pltpu.VMEM((1 + 2 * B_SIZE, 8, BX), f32),
             pltpu.VMEM((CHUNKS, A_SIZE, SLOTS, CH, BX), f32),
             pltpu.VMEM((CHUNKS, A_SIZE, SLOTS, CH, BX), f32),
@@ -652,8 +653,8 @@
     out_hbm, drag_out_ref, surface_out_ref, sens_out_ref, stage, sems, small_sems,
 ):
     small = ((drag_ref, drag_out_ref), (surface_ref, surface_out_ref), (sens_ref, sens_out_ref))
-    puts = [pltpu.make_async_copy(src, dst, small_sems.at[i]) for i, (src, dst) in enumerate(small)]
-    for c in puts:
+    extra = [pltpu.make_async_copy(src, dst, small_sems.at[i]) for i, (src, dst) in enumerate(small)]
+    for c in extra:
         c.start()
     for slot in range(SLOTS):
         levels = count_ref[slot]
@@ -665,10 +666,10 @@
                     less = jnp.where(levels == k + 1, bed, jnp.where(levels > k, press, 0.0))
                     stage[slot, c, k] = mixed_ref[slot, c, k] - less
                 part = (slot, c, pl.ds(piece * LEV // PIECES, LEV // PIECES))
-                puts.append(pltpu.make_async_copy(stage.at[part], out_hbm.at[part], sems.at[len(puts) - len(small)]))
-                puts[-1].start()
-    for c in puts:
+                pltpu.make_async_copy(stage.at[part], out_hbm.at[part], sems.at[0]).start()
+    for c in extra:
         c.wait()
+    pltpu.make_async_copy(stage, out_hbm, sems.at[0]).wait()
 
 
 def final_call(level_count, mixed, press, pull, drag_grad, surface, sens):
@@ -685,7 +686,7 @@
         ),
         in_specs=[vmem] * 7,
         out_specs=(pl.BlockSpec(memory_space=pltpu.HBM),) * 4,
-        scratch_shapes=[pltpu.VMEM(deep, f32), pltpu.SemaphoreType.DMA((SLOTS * 2 * PIECES,)), pltpu.SemaphoreType.DMA((3,))],
+        scratch_shapes=[pltpu.VMEM(deep, f32), pltpu.SemaphoreType.DMA((1,)), pltpu.SemaphoreType.DMA((3,))],
         compiler_params=pltpu.CompilerParams(vmem_limit_bytes=24 * 2**20),
         name="pressure_correction",
     )(level_count, mixed, press, pull, drag_grad, surface, sens)

time: 49 us -> 48.5 us (0.990)
  Pallas kernels: 48.2 us -> 47.7 us
where the time goes in v6:
time: 48.5 us; the launch traced here: 48.4 us
  Pallas kernels  47.7 us (98%)
  between operations  0.66 us (1%)
    pallas_call x1, Pallas kernels, main_call(): pl.pallas_call(main_kernel, out_shape=(pltpu.VMEM((SLOTS, 2, LEV, BY, BX)...  44.3 us
    pallas_call x1, Pallas kernels, final_call(): pl.pallas_call(final_kernel, out_shape=(jax.ShapeDtypeStruct(deep, f32),...  3.38 us

profile of v6, /device:TPU:1, one launch (start us, length us, event | category | flops | bytes accessed | tf_op | source)
XLA Modules:
  0.0 48.4 jit_solution(10362639561699435911)
XLA Ops:
  0.6 0.0 copy-start
  0.6 44.3 %columns_and_surface.1 = (f32[4,2,62,32,128]{4,3,2,1,0:T(8,128)S(1)}, f32[4,2,32,128]{3,2,1,0:T(8,128)S(1)}, f32[4,2,32,128]{3,2,1,0:T(8,128)S(1)}, f32[4,32,128...) custom-call(s32[4]{0:T(128)} %ids_hbm.1, s32[4,32,128]{2,1,0:T(8,128)} %count_ref.1, ...), custom_call_target="tpu_custom_call" | custom-call | tf_op jit(solution)/shard_map/columns_and_surface/pallas_call | solution.py:570
  45.0 0.0 copy-done
  45.0 3.4 %pressure_correction.1 = (f32[4,2,62,32,128]{4,3,2,1,0:T(8,128)}, f32[4,32,128]{2,1,0:T(8,128)}, f32[32,256]{1,0:T(8,128)}, f32[32,256]{1,0:T(8,128)}) custom-call(s32[4,32,128]{2,1,0:T(8,128)S(1)} %copy-done, f32[4,2,62,32,128]{4,3,2,1,0:T(8,128)S(1)} %get-tuple-element.10.mixed_ref, f32[4,2,32,128]{3,2,1,0:T(8,128)S(1)} %get-tuple-element.11.press_ref, ...), custom_call_target="tpu_custom_call" | custom-call | tf_op jit(solution)/shard_map/pressure_correction/pallas_call | solution.py:679
Async XLA Ops:
  0.6 44.3 %copy-start = (s32[4,32,128]{2,1,0:T(8,128)S(1)}, s32[4,32,128]{2,1,0:T(8,128)}, u32[]{:S(2)}) copy-start(s32[4,32,128]{2,1,0:T(8,128)} %count_ref.1) | copy-start | bytes 196612

commit v7 on v6

--- a/solution.py
+++ b/solution.py
@@ -264,9 +264,10 @@
 
     small[0].wait()
     small[1].wait()
-    id_row = jnp.full((8, BX), -1, jnp.int32)
+    lane1 = lax.broadcasted_iota(jnp.int32, (1, BX), 1)
+    id_row = jnp.full((1, BX), -1, jnp.int32)
     for s in range(SLOTS):
-        id_row = jnp.where(lane8 == s, ids_ref[s], id_row)
+        id_row = jnp.where(lane1 == s, ids_ref[s], id_row)
         levels_ref[s] = count_ref[s] * jnp.where(ids_ref[s] < 256, 1, 0)
     idbuf[0] = id_row
     for q in range(CHUNKS):
@@ -587,7 +588,7 @@
             pltpu.VMEM((SLOTS, BY, BX), f32),
             pltpu.VMEM((BY, 2 * BX), f32),
             pltpu.VMEM((BY, 2 * BX), i32),
-            pltpu.VMEM((A_SIZE, 8, BX), i32),
+            pltpu.VMEM((A_SIZE, 1, BX), i32),
             pltpu.VMEM((2 * B_SIZE, BX), i32),
             pltpu.VMEM((A_SIZE, BX), i32),
             pltpu.SMEM((2 * B_SIZE, BX), i32),

time: 48.5 us -> 48.2 us (level)
  no operation moved by 1% of the time
where the time goes in v7:
time: 48.2 us; the launch traced here: 48.1 us
  Pallas kernels  47.4 us (98%)
  between operations  0.66 us (1%)
    pallas_call x1, Pallas kernels, main_call(): pl.pallas_call(main_kernel, out_shape=(pltpu.VMEM((SLOTS, 2, LEV, BY, BX)...  44 us
    pallas_call x1, Pallas kernels, final_call(): pl.pallas_call(final_kernel, out_shape=(jax.ShapeDtypeStruct(deep, f32),...  3.38 us

profile of v7, /device:TPU:1, one launch (start us, length us, event | category | flops | bytes accessed | tf_op | source)
XLA Modules:
  0.0 48.1 jit_solution(8085163577055809048)
XLA Ops:
  0.6 0.0 copy-start
  0.6 44.0 %columns_and_surface.1 = (f32[4,2,62,32,128]{4,3,2,1,0:T(8,128)S(1)}, f32[4,2,32,128]{3,2,1,0:T(8,128)S(1)}, f32[4,2,32,128]{3,2,1,0:T(8,128)S(1)}, f32[4,32,128...) custom-call(s32[4]{0:T(128)} %ids_hbm.1, s32[4,32,128]{2,1,0:T(8,128)} %count_ref.1, ...), custom_call_target="tpu_custom_call" | custom-call | tf_op jit(solution)/shard_map/columns_and_surface/pallas_call | solution.py:571
  44.7 0.0 copy-done
  44.7 3.4 %pressure_correction.1 = (f32[4,2,62,32,128]{4,3,2,1,0:T(8,128)}, f32[4,32,128]{2,1,0:T(8,128)}, f32[32,256]{1,0:T(8,128)}, f32[32,256]{1,0:T(8,128)}) custom-call(s32[4,32,128]{2,1,0:T(8,128)S(1)} %copy-done, f32[4,2,62,32,128]{4,3,2,1,0:T(8,128)S(1)} %get-tuple-element.10.mixed_ref, f32[4,2,32,128]{3,2,1,0:T(8,128)S(1)} %get-tuple-element.11.press_ref, ...), custom_call_target="tpu_custom_call" | custom-call | tf_op jit(solution)/shard_map/pressure_correction/pallas_call | solution.py:680
Async XLA Ops:
  0.6 44.1 %copy-start = (s32[4,32,128]{2,1,0:T(8,128)S(1)}, s32[4,32,128]{2,1,0:T(8,128)}, u32[]{:S(2)}) copy-start(s32[4,32,128]{2,1,0:T(8,128)} %count_ref.1) | copy-start | bytes 196612
